TPU v7x, 512 devices: a whole 4x4x16 slice. The times are simulated.
512 devices in a mesh: elem: 64 (over x, z_hi, y, core), lev: 8 (over z_lo).
Axes of the slice: x: 4, y: 4, z: 16 (z_hi: 2, z_lo: 8; z = z_hi * 8 + z_lo), core: 2. Of those that a mesh axis runs over, the one named last changes fastest.
Arguments:
- zonal_wind: float32 [128, 16, 8192], P('lev', None, 'elem'), may hold values from -6 to 6
- meridional_wind: float32 [128, 16, 8192], P('lev', None, 'elem'), may hold values from -6 to 6
- vertical_wind: float32 [128, 16, 8192], P('lev', None, 'elem'), may hold values from -6 to 6
- pressure: float32 [128, 16, 8192], P('lev', None, 'elem'), may hold values from -6 to 6
- geopotential: float32 [128, 16, 8192], P('lev', None, 'elem'), may hold values from -6 to 6
- layer_mass: float32 [128, 16, 8192], P('lev', None, 'elem'), may hold values from 0.5 to 2
- stiffness: float32 [128, 16, 8192], P(None, 'lev', 'elem'), may hold values from 4 to 1024
- elem_order: int32 [64, 128], P('elem'), may hold values from 0 to 127, each once within a row
Outputs:
- zonal_out: float32 [128, 16, 8192], P('lev', None, 'elem')
- meridional_out: float32 [128, 16, 8192], P('lev', None, 'elem')
- vertical_out: float32 [128, 16, 8192], P('lev', None, 'elem')
- pressure_out: float32 [128, 16, 8192], P('lev', None, 'elem')
- geopotential_out: float32 [128, 16, 8192], P('lev', None, 'elem')
Inputs may be any that keep to these rules, and one draw needn't show every extreme that they name: `elem_order`: each row is a permutation of the positions 0 .. 127 of its strip.
All inputs are finite; a program needn't handle non-finite values.
Results may differ from a plain program's by a relative error of at most 0.0003.
Values sent between devices are 32-bit elements; how exact they have to be, the bound alone decides.
No kernel may reach another device: no remote copies, remote signals or barrier semaphores. Data moves between devices by JAX's collectives and lax.ppermute only.
A program may use at most 128 MiB of HBM per device.

v0:
```python
import functools
import math

import jax
import jax.numpy as jnp
import numpy as np
from jax import lax
from jax.experimental import pallas as pl
from jax.experimental.pallas import tpu as pltpu
from jax.sharding import PartitionSpec as P

SUBSTEPS = 3
SPEED = 0.12
DRIFT1 = 0.1
DRIFT2 = 0.06
RATE = 2.0
F32 = jnp.float32
LANES = 128
NL = 16
ROWS = 36
PAD = 40


def tables():
    points = np.array([-1.0, -1.0 / math.sqrt(5.0), 1.0 / math.sqrt(5.0), 1.0])
    quad = [1.0 / 6.0, 5.0 / 6.0, 5.0 / 6.0, 1.0 / 6.0]
    d = np.zeros((4, 4))
    for t in range(4):
        for s in range(4):
            if t == s:
                d[t, s] = sum(1.0 / (points[t] - points[o]) for o in range(4) if o != t)
            else:
                top = math.prod(points[t] - points[o] for o in range(4) if o != t)
                low = math.prod(points[s] - points[o] for o in range(4) if o != s)
                d[t, s] = top / (low * (points[t] - points[s]))
    d[np.abs(d) < 1e-12] = 0.0
    return [[float(x) for x in row] for row in d], [float(a * b) for a in quad for b in quad]


D, WEIGHT = tables()


def lin(coeffs, values):
    total = None
    for c, v in zip(coeffs, values):
        if c != 0.0:
            total = c * v if total is None else total + c * v
    return total


def up(x):
    return pltpu.roll(x, LANES - 1, 1)


def down(x):
    return pltpu.roll(x, 1, 1)


def sew(row):
    last = row[3] + up(row[0])
    return [down(last), row[1], row[2], last]


def rows(ref, n):
    return ref[n * NL : (n + 1) * NL, :]


def put(ref, n, value):
    ref[n * NL : (n + 1) * NL, :] = value


def dx(get, i, j):
    return lin(D[i], [get(k * 4 + j) for k in range(4)])


def dy(get, i, j):
    return lin(D[j], [get(i * 4 + k) for k in range(4)])


def three(ref, base):
    a, b, c = (rows(ref, base + k) for k in range(3))
    return [down(c), a, b, c]


def place():
    core = lax.rem(lax.axis_index("elem"), 2)
    return core, (1 - 2 * core).astype(F32)


def inverse_of(order_ref):
    order = order_ref[...].astype(F32)
    across = jnp.broadcast_to(order, (LANES, LANES))
    along = across.T
    lane = lax.broadcasted_iota(jnp.int32, (LANES, LANES), 1).astype(F32)
    slot = lax.broadcasted_iota(jnp.int32, (LANES, LANES), 0).astype(F32)
    return jnp.sum(jnp.where(along == lane, slot, 0.0), axis=0, keepdims=True).astype(jnp.int32)


def pick(values, index):
    return jnp.take_along_axis(values, index, axis=1, mode="promise_in_bounds")


def stage_a(sg, src, p, m, r, dst, ta, tb):
    for f in range(4):
        if f < 2:
            get = functools.partial(rows, p)
        else:
            get = functools.partial(rows, src[f])
        for i in range(4):
            row = []
            for j in range(4):
                if f == 0:
                    t = (-SPEED * sg) * dx(get, i, j)
                elif f == 1:
                    t = -SPEED * dy(get, i, j)
                else:
                    t = -((DRIFT1 * sg) * dx(get, i, j) + DRIFT2 * dy(get, i, j))
                row.append(rows(m, i * 4 + j) * t)
            row = sew(row)
            for j in range(4):
                n = i * 4 + j
                own = rows(src[f], n)
                if i in (1, 2):
                    put(dst[f], n, own + rows(r, n) * row[j])
                else:
                    put(dst[f], n, own)
                    if j > 0:
                        put(ta if i == 3 else tb, f * 3 + j - 1, row[j])


def k_init(order, u_in, v_in, w_in, p_in, g_in, lm_in, u, v, w, g, p, m, r, ta, tb, us, vs, ws, gs):
    core, sg = place()
    index = jnp.broadcast_to(inverse_of(order), (NL, LANES))
    for src, dst in ((p_in, p), (lm_in, m), (u_in, us), (v_in, vs), (w_in, ws), (g_in, gs)):
        for i in range(4):
            for j in range(4):
                start = jnp.where(core == 1, (3 - i) * 4 + j, i * 4 + j)
                value = pick(src[pl.ds(start, NL, stride=16), :], index)
                if dst is m:
                    value = value * WEIGHT[i * 4 + j]
                put(dst, i * 4 + j, value)
    for i in range(4):
        row = sew([rows(m, i * 4 + j) for j in range(4)])
        for j in range(4):
            if i in (1, 2):
                put(r, i * 4 + j, 1.0 / row[j])
            else:
                put(r, i * 4 + j, row[j])
                if j > 0:
                    put(ta if i == 3 else tb, 12 + j - 1, row[j])
    stage_a(sg, (us, vs, ws, gs), p, m, r, (u, v, w, g), ta, tb)


def k_b(first, *refs):
    if first:
        u, v, w, g, m, r, ta, ra, tb, f3, bm, r3 = refs
        own, got = three(ta, 12), three(ra, 12)
        for j in range(4):
            put(r3, j, 1.0 / (own[j] + got[j]))
        rr = lambda j: rows(r3, j)
    else:
        u, v, w, g, r, ta, ra, tb, f3, bm = refs
        rr = lambda j: rows(r, 12 + j)
    _, sg = place()
    for f, field in enumerate((u, v, w, g)):
        own, got = three(ta, f * 3), three(ra, f * 3)
        for j in range(4):
            put(f3, f * 4 + j, rows(field, 12 + j) + rr(j) * (own[j] + got[j]))
    for j in range(4):
        along = lin(D[0], [rows(u, j), rows(u, 4 + j), rows(u, 8 + j), rows(f3, j)])
        across = dy(functools.partial(rows, v), 0, j)
        put(bm, 12 + j, sg * along + across)
    for k in range(12):
        put(bm, k, rows(tb, k))
    if first:
        for j in range(4):
            put(bm, 16 + j, rows(m, j))


def k_c(first, *refs):
    if first:
        u, v, w, g, p, m, r, r3, f3, tb, rb, uo, vo, wo, go, po, dm, ro, mo = refs
        own, got = three(tb, 12), sew([rows(rb, 16 + j) for j in range(4)])
        for j in range(4):
            put(ro, j, 1.0 / (own[j] + got[j]))
            put(ro, 12 + j, rows(r3, j))
            put(mo, j, rows(rb, 16 + j))
            for i in (1, 2):
                put(ro, i * 4 + j, rows(r, i * 4 + j))
        r, mn = ro, mo
    else:
        u, v, w, g, p, m, r, mn, f3, tb, rb, uo, vo, wo, go, po, dm = refs
    _, sg = place()
    inc = []
    for f, (field, out) in enumerate(((u, uo), (v, vo), (w, wo), (g, go))):
        own, got = three(tb, f * 3), three(rb, f * 3)
        part = []
        for j in range(4):
            add = rows(r, j) * (own[j] + got[j])
            part.append(add)
            put(out, j, rows(field, j) + add)
            put(out, 12 + j, rows(f3, f * 4 + j))
            for i in (1, 2):
                put(out, i * 4 + j, rows(field, i * 4 + j))
        if f < 2:
            inc.append(part)
    other = []
    for j in range(4):
        t = rows(rb, 12 + j) - (sg * D[0][0]) * inc[0][j] + lin(D[j], inc[1])
        other.append(rows(mn, j) * (-SPEED * t))
    other = sew(other)
    gu, gv = functools.partial(rows, uo), functools.partial(rows, vo)
    for i in range(4):
        row = sew([rows(m, i * 4 + j) * (-SPEED * (sg * dx(gu, i, j) + dy(gv, i, j))) for j in range(4)])
        for j in range(4):
            n = i * 4 + j
            total = row[j] + other[j] if i == 0 else row[j]
            put(po, n, rows(p, n) + rows(r, n) * total)
            if i == 3 and j > 0:
                put(dm, j - 1, row[j])


def level(ref, k):
    return jnp.concatenate([ref[pl.ds(k, 8, stride=32), :], ref[pl.ds(16 + k, 8, stride=32), :]], 0)


def node_of(ref, n):
    return ref[pl.ds((n % 2) * 8 + n // 2, NL, stride=16), :]


def k_d(p, w, r, rd, wu, pu, wd, pd, po, vm):
    me = lax.axis_index("lev")
    got = three(rd, 0)
    for n in range(12):
        put(po, n, rows(p, n))
    for j in range(4):
        put(po, 12 + j, rows(p, 12 + j) + rows(r, 12 + j) * got[j])
    su = sd = None
    for k in range(NL):
        wk, pk = level(w, k), level(po, k)
        a = rows(wu, k) * wk + rows(pu, k) * pk
        b = rows(wd, k) * wk + rows(pd, k) * pk
        su = a if su is None else su + a
        sd = b if sd is None else sd + b
    low, high = level(po, 0), level(po, NL - 1)
    for c in range(8):
        above = c > me
        vm[c * 32 : c * 32 + 16, :] = jnp.where(above, su, sd)
        vm[c * 32 + 16 : c * 32 + 32, :] = jnp.where(above, high, low)


def solve(p, w, rv, ia, hr, rh, cp, cc, edge, s_out, p_out):
    me = lax.axis_index("lev")
    low, high = level(p, 0), level(p, NL - 1)
    from_below = -rows(edge, 0) * low
    from_above = rows(edge, 1) * high
    for c in range(8):
        part = rows(cc, 2 * c) * rows(rv, 2 * c) + rows(cc, 2 * c + 1) * rows(rv, 2 * c + 1)
        from_below = from_below + jnp.where(c < me, part, 0.0)
        from_above = from_above + jnp.where(c > me, part, 0.0)
    prev = rv[pl.ds(pl.multiple_of(jnp.maximum(me - 1, 0) * 32 + 16, 16), 16), :]
    then = rv[pl.ds(pl.multiple_of(jnp.minimum(me + 1, 7) * 32 + 16, 16), 16), :]
    prev = jnp.where(me > 0, prev, 0.0)
    then = jnp.where(me < 7, then, 0.0)
    d = []
    last = from_below
    for k in range(NL):
        below = level(p, k - 1) if k > 0 else prev
        above = level(p, k + 1) if k < NL - 1 else then
        q = level(w, k) * rows(ia, k) - (above - below) * rows(hr, k)
        last = rows(cp, k) * (q + last)
        d.append(last)
    s = (d[NL - 1] + rows(cp, NL - 1) * from_above) * rows(edge, 2)
    after = from_above + rows(edge, 4) * s
    for k in range(NL - 1, -1, -1):
        put(s_out, k, s)
        if k > 0:
            nxt = d[k - 1] + rows(cp, k - 1) * s
        else:
            nxt = from_below + rows(edge, 3) * s
        put(p_out, k, level(p, k) - rows(rh, k) * (after - nxt))
        after, s = s, nxt


def k_e(p, w, g, u, v, rv, ia, hr, rh, cp, cc, edge, m, r, uo, vo, wo, go, po, ta, tb, ss, ps, ws, gs):
    _, sg = place()
    solve(p, w, rv, ia, hr, rh, cp, cc, edge, ss, ps)
    for n in range(16):
        s = node_of(ss, n)
        put(ws, n, s)
        put(gs, n, rows(g, n) + RATE * s)
        put(po, n, node_of(ps, n))
    stage_a(sg, (u, v, ws, gs), po, m, r, (uo, vo, wo, go), ta, tb)


def k_out(order, p, w, g, u, v, rv, ia, hr, rh, cp, cc, edge, uo, vo, wo, po, go, ss, ps):
    core, _ = place()
    solve(p, w, rv, ia, hr, rh, cp, cc, edge, ss, ps)
    index = jnp.broadcast_to(order[...], (NL, LANES))
    for i in range(4):
        for j in range(4):
            n = i * 4 + j
            start = jnp.where(core == 1, (3 - i) * 4 + j, n)
            s = node_of(ss, n)
            for out, value in (
                (uo, rows(u, n)),
                (vo, rows(v, n)),
                (wo, s),
                (po, node_of(ps, n)),
                (go, rows(g, n) + RATE * s),
            ):
                out[pl.ds(start, NL, stride=16), :] = pick(value, index)


def k_col(order, st, out, a_s, ia_s):
    index = jnp.broadcast_to(inverse_of(order), (NL, LANES))
    for k in range(16):
        a = pick(st[k * 16 : k * 16 + 16, :], index)
        a_s[k * 16 : k * 16 + 16, :] = a
        ia_s[k * 16 : k * 16 + 16, :] = 1.0 / a
    one = jnp.ones((2, LANES), F32)
    zero = jnp.zeros((2, LANES), F32)
    pair = lambda ref, k: ref[2 * k : 2 * k + 2, :]
    th, de = one, one
    th_last, rho = [], [one]
    for k in range(128):
        de = de + th * pair(ia_s, k)
        th = th + de
        if k % 16 == 15:
            th_last.append(th)
            rho.append(de / th)
    ps, de = one, one
    ps_first, sig = [None] * 8, [None] * 9
    sig[8] = one
    for k in range(127, -1, -1):
        de = de + ps * pair(ia_s, k)
        ps = ps + de
        if k % 16 == 0:
            ps_first[k // 16] = ps
            sig[k // 16] = de / ps
    inv_th = [1.0 / x for x in th_last]
    inv_ps = [1.0 / x for x in ps_first]
    half = lambda k: 0.5 * jnp.sqrt(pair(ia_s, k))
    lo_half = [half(16 * c + 16) if c < 7 else zero for c in range(8)]
    hi_half = [half(16 * c - 1) if c > 0 else zero for c in range(8)]
    for b in range(8):
        def send(t, value):
            out[b * 80 + 2 * t : b * 80 + 2 * t + 2, :] = value

        for k in range(16):
            send(k, pair(a_s, b * 16 + k))
        for c in range(8):
            cs = cq = zero
            if c < b:
                cs = th_last[c] * inv_th[b - 1]
                if c < b - 1:
                    cq = cs * lo_half[c]
            elif c > b:
                cs = ps_first[c] * inv_ps[b + 1]
                if c > b + 1:
                    cq = -cs * hi_half[c]
            send(16 + 2 * c, cs)
            send(17 + 2 * c, cq)
        send(32, rho[b])
        send(33, sig[b + 1])
        send(34, hi_half[b])
        send(35, lo_half[b])
        for t in range(ROWS, PAD):
            send(t, zero)


def k_stat(got, ia, hr, rh, cp, wu, pu, wd, pd, cc, edge, scr, tu_s, td_s):
    core, _ = place()
    for s in range(8):
        src = jnp.where(core == 1, s ^ 6, s)
        scr[s * 80 : (s + 1) * 80, :] = got[pl.ds(pl.multiple_of(src * 80, 8), 80), :]

    def row(t):
        return jnp.concatenate([scr[pl.ds(2 * t + e, 8, stride=80), :] for e in range(2)], 0)

    for k in range(NL):
        a = row(k)
        ra = 1.0 / a
        root = jnp.sqrt(a)
        put(ia, k, ra)
        put(rh, k, 0.5 * root)
        put(hr, k, 0.5 * (ra * root))
    for t in range(16):
        put(cc, t, row(16 + t))
    rho, sig, h_lo, h_hi = row(32), row(33), row(34), row(35)
    th, de = jnp.ones_like(rho), rho
    for k in range(NL):
        de = de + th * rows(ia, k)
        new = th + de
        put(cp, k, th / new)
        put(tu_s, k, th)
        th = new
    inv_th = 1.0 / th
    ps, de = jnp.ones_like(rho), sig
    for k in range(NL - 1, -1, -1):
        de = de + ps * rows(ia, k)
        put(td_s, k, ps)
        ps = ps + de
    inv_ps = 1.0 / ps
    for ref, inv in ((tu_s, inv_th), (td_s, inv_ps)):
        for k in range(NL):
            put(ref, k, rows(ref, k) * inv)
    cpm, cqp = 1.0 - rho, 1.0 - sig
    for ref, wt, pt, in ((tu_s, wu, pu), (td_s, wd, pd)):
        for k in range(NL):
            put(wt, k, rows(ref, k) * rows(ia, k))
            value = None
            if k < NL - 1:
                value = rows(ref, k + 1) * rows(hr, k + 1)
            elif ref is td_s:
                value = rows(ref, k) * cqp * h_hi
            else:
                value = jnp.zeros_like(rho)
            if k > 0:
                value = value - rows(ref, k - 1) * rows(hr, k - 1)
            elif ref is tu_s:
                value = value - rows(ref, 0) * cpm * h_lo
            put(pt, k, value)
    put(edge, 0, cpm * h_lo)
    put(edge, 1, cqp * h_hi)
    put(edge, 2, 1.0 / (1.0 - rows(cp, NL - 1) * cqp))
    put(edge, 3, cpm)
    put(edge, 4, cqp)


def call(kernel, name, args, outs, scratch=()):
    vmem = pl.BlockSpec(memory_space=pltpu.VMEM)
    return pl.pallas_call(
        kernel,
        out_shape=[jax.ShapeDtypeStruct((n * NL, LANES), F32) for n in outs],
        in_specs=[vmem] * len(args),
        out_specs=[vmem] * len(outs),
        scratch_shapes=[pltpu.VMEM((n * NL, LANES), F32) for n in scratch],
        name=name,
    )(*args)


def body(zonal, meridional, vertical, pressure, geopotential, layer_mass, stiffness, order):
    count = lax.axis_size("elem")
    mates = [(i, i ^ 1) for i in range(count)]
    others = [(i, (i + 1) % count if i % 2 else (i - 1) % count) for i in range(count)]
    flat = lambda x: x.reshape(-1, LANES)
    u, v, w, p, g, lm = (flat(x) for x in (zonal, meridional, vertical, pressure, geopotential, layer_mass))

    def swap_levels(x):
        return lax.all_to_all(x.reshape(8, -1, LANES), "lev", 0, 0, tiled=True).reshape(-1, LANES)

    (sent,) = call(k_col, "col", [order, flat(stiffness)], [40], [16, 16])
    got = swap_levels(sent)
    u, v, w, g, p, m, r, ta, tb = call(
        k_init, "init", [order, u, v, w, p, g, lm], [16] * 7 + [15, 15], [16] * 4
    )
    mn = r3 = None
    statics = None
    for step in range(SUBSTEPS):
        first = step == 0
        ra = lax.ppermute(ta, "elem", mates)
        if first:
            f3, bm, r3 = call(functools.partial(k_b, True), "b1", [u, v, w, g, m, r, ta, ra, tb], [16, 20, 4])
        else:
            f3, bm = call(functools.partial(k_b, False), "b", [u, v, w, g, r, ta, ra, tb], [16, 16])
        rb = lax.ppermute(bm, "elem", others)
        if first:
            u, v, w, g, p, dm, r, mn = call(
                functools.partial(k_c, True),
                "c1",
                [u, v, w, g, p, m, r, r3, f3, tb, rb],
                [16] * 5 + [3, 16, 4],
            )
        else:
            u, v, w, g, p, dm = call(
                functools.partial(k_c, False), "c", [u, v, w, g, p, m, r, mn, f3, tb, rb], [16] * 5 + [3]
            )
        rd = lax.ppermute(dm, "elem", mates)
        if first:
            ia, hr, rh, cp, wu, pu, wd, pd, cc, edge = call(
                k_stat, "stat", [got], [16] * 8 + [16, 5], [40, 16, 16]
            )
            statics = [ia, hr, rh, cp, cc, edge]
        p, vm = call(k_d, "d", [p, w, r, rd, wu, pu, wd, pd], [16, 16])
        rv = swap_levels(vm)
        if step < SUBSTEPS - 1:
            u, v, w, g, p, ta, tb = call(
                k_e, "e", [p, w, g, u, v, rv] + statics + [m, r], [16] * 5 + [12, 12], [16] * 4
            )
        else:
            outs = call(k_out, "out", [order, p, w, g, u, v, rv] + statics, [16] * 5, [16] * 2)
    return tuple(x.reshape(zonal.shape) for x in outs)


def solution(mesh):
    fields = P("lev", None, "elem")
    return jax.shard_map(
        body,
        mesh=mesh,
        in_specs=(fields,) * 6 + (P(None, "lev", "elem"), P("elem", None)),
        out_specs=(fields,) * 5,
        check_vma=False,
    )
```

profile of v0, /device:TPU:32, one launch (start us, length us, event | category | flops | bytes accessed | tf_op | source)
XLA Modules:
  0.0 196.3 jit_solution(4852723768079820977)
XLA Ops:
  0.6 2.2 %col.1 = f32[640,128]{1,0:T(8,128)} custom-call(s32[1,128]{1,0:T(1,128)} %order.5, f32[256,128]{1,0:T(8,128)} %bitcast.28), custom_call_target="tpu_custom_call" | custom-call | tf_op jit(solution)/shard_map/col/pallas_call | solution.py:433
  2.9 12.6 %all-to-all-start = ((f32[8,80,128]{2,1,0:T(8,128)}), f32[8,80,128]{2,1,0:T(8,128)S(1)}, u32[]{:S(2)}, u32[]{:S(2)}) async-start(f32[8,80,128]{2,1,0:T(8,128)} %bitcast.21), calls=%async_computation | async-start | bytes 655360 | tf_op jit(solution)/shard_map/all_to_all | solution.py:451
  15.5 2.9 %init.1 = (f32[256,128]{1,0:T(8,128)}, f32[256,128]{1,0:T(8,128)}, f32[256,128]{1,0:T(8,128)}, f32[256,128]{1,0:T(8,128)}, f32[256,128]{1,0:T(8,128)}, /*index=5...) custom-call(s32[1,128]{1,0:T(1,128)} %order.5, f32[256,128]{1,0:T(8,128)} %bitcast.29, ...), custom_call_target="tpu_custom_call" | custom-call | tf_op jit(solution)/shard_map/init/pallas_call | solution.py:433
  18.4 1.9 collective-permute-start
  20.3 1.5 collective-permute-done.refs_7_
  22.5 2.2 %b1.1 = (f32[256,128]{1,0:T(8,128)}, f32[320,128]{1,0:T(8,128)}, f32[64,128]{1,0:T(8,128)}) custom-call(f32[256,128]{1,0:T(8,128)} %get-tuple-element.76.refs_0_, f32[256,128]{1,0:T(8,128)} %get-tuple-element.77.refs_1_, f32[256,128]{1,0:T(8,128)} %get-tuple-element.78.refs_2_, f32[256,128]{1,0:T(8,128)} %get-tuple-element.79.refs_3_, ...), custom_call_target="tpu_custom_call" | custom-call | tf_op jit(solution)/shard_map/b1/pallas_call | solution.py:433
  24.6 12.6 %collective-permute-start.1 = (f32[320,128]{1,0:T(8,128)}, f32[320,128]{1,0:T(8,128)S(1)}, u32[]{:S(2)}, u32[]{:S(2)}) collective-permute-start(f32[320,128]{1,0:T(8,128)} %get-tuple-element.87), channel_id=1, source_target_pairs={{0,504},{8,16},{16,8},{24,32},{32,24},{40,48},{48,40},{56,64},{64,... | collective-permute-start | bytes 491528 | tf_op jit(solution)/shard_map/ppermute | solution.py:467
  37.3 7.5 %collective-permute-done.1.refs_10_ = f32[320,128]{1,0:T(8,128)S(1)} collective-permute-done((f32[320,128]{1,0:T(8,128)}, f32[320,128]{1,0:T(8,128)S(1)}, u32[]{:S(2)}, u32[]{:S(2)}) %collective-permute-start.1) | collective-permute-done | bytes 163872 | tf_op jit(solution)/shard_map/ppermute | solution.py:467
  45.4 2.5 %c1.1 = (f32[256,128]{1,0:T(8,128)}, f32[256,128]{1,0:T(8,128)}, f32[256,128]{1,0:T(8,128)}, f32[256,128]{1,0:T(8,128)}, f32[256,128]{1,0:T(8,128)}, /*index=5*/...) custom-call(f32[256,128]{1,0:T(8,128)} %get-tuple-element.76.refs_0_, f32[256,128]{1,0:T(8,128)} %get-tuple-element.77.refs_1_, ...), custom_call_target="tpu_custom_call" | custom-call | tf_op jit(solution)/shard_map/c1/pallas_call | solution.py:433
  48.0 1.9 collective-permute-start.2
  50.6 2.1 %stat.1 = (f32[256,128]{1,0:T(8,128)}, f32[256,128]{1,0:T(8,128)}, f32[256,128]{1,0:T(8,128)}, f32[256,128]{1,0:T(8,128)}, f32[256,128]{1,0:T(8,128)}, /*index=5...) custom-call(f32[640,128]{1,0:T(8,128)} %bitcast.20), custom_call_target="tpu_custom_call" | custom-call | tf_op jit(solution)/shard_map/stat/pallas_call | solution.py:433
  53.3 2.1 %d.3 = (f32[256,128]{1,0:T(8,128)}, f32[256,128]{1,0:T(8,128)}) custom-call(f32[256,128]{1,0:T(8,128)} %get-tuple-element.88.p, f32[256,128]{1,0:T(8,128)} %get-tuple-element.89.w, f32[256,128]{1,0:T(8,128)} %get-tuple-element.90.r.refs_4_.refs_6_, f32[48,128]{1,0:T(8,128)} %copy-done.7, f32[256,128]{1,0:T(8,128)} %get-tuple-element.92.wu, ...), custom_call_target="tpu_custom_call" | custom-call | tf_op jit(solution)/shard_map/d/pallas_call | solution.py:433
  55.4 25.1 %all_to_all.20 = f32[8,32,128]{2,1,0:T(8,128)} all-to-all(f32[8,32,128]{2,1,0:T(8,128)} %bitcast.26), channel_id=1, replica_groups=mesh['elem'=64,'lev'=8] {'lev'}, dimensions={0} | all-to-all | bytes 262144 | tf_op jit(solution)/shard_map/all_to_all | solution.py:451
  80.5 3.0 %e.2 = (f32[256,128]{1,0:T(8,128)}, f32[256,128]{1,0:T(8,128)}, f32[256,128]{1,0:T(8,128)}, f32[256,128]{1,0:T(8,128)}, f32[256,128]{1,0:T(8,128)}, /*index=5*/f32[192,128]{1,0:T(8,128)}, f32[192,128]{1,0:T(8,128)}) custom-call(f32[256,128]{1,0:T(8,128)} %get-tuple-element.96.p, f32[256,128]{1,0:T(8,128)} %get-tuple-element.89.w, ...), custom_call_target="tpu_custom_call" | custom-call | tf_op jit(solution)/shard_map/e/pallas_call | solution.py:433
  83.5 1.9 collective-permute-start.3
  87.5 2.1 %b.2 = (f32[256,128]{1,0:T(8,128)}, f32[256,128]{1,0:T(8,128)}) custom-call(f32[256,128]{1,0:T(8,128)} %get-tuple-element.107.refs_0_, f32[256,128]{1,0:T(8,128)} %get-tuple-element.108.refs_1_, f32[256,128]{1,0:T(8,128)} %get-tuple-element.109.refs_2_, f32[256,128]{1,0:T(8,128)} %get-tuple-element.110.refs_3_, ...), custom_call_target="tpu_custom_call" | custom-call | tf_op jit(solution)/shard_map/b/pallas_call | solution.py:433
  89.5 12.5 %collective-permute-start.4 = (f32[256,128]{1,0:T(8,128)}, f32[256,128]{1,0:T(8,128)S(1)}, u32[]{:S(2)}, u32[]{:S(2)}) collective-permute-start(f32[256,128]{1,0:T(8,128)} %get-tuple-element.116), channel_id=1, source_target_pairs={{0,504},{8,16},{16,8},{24,32},{32,24},{40,48},{48,40},{56,64},{64,... | collective-permute-start | bytes 393224 | tf_op jit(solution)/shard_map/ppermute | solution.py:467
  102.0 10.3 %collective-permute-done.4.refs_10_ = f32[256,128]{1,0:T(8,128)S(1)} collective-permute-done((f32[256,128]{1,0:T(8,128)}, f32[256,128]{1,0:T(8,128)S(1)}, u32[]{:S(2)}, u32[]{:S(2)}) %collective-permute-start.4) | collective-permute-done | bytes 131104 | tf_op jit(solution)/shard_map/ppermute | solution.py:467
  113.0 2.4 %c.2 = (f32[256,128]{1,0:T(8,128)}, f32[256,128]{1,0:T(8,128)}, f32[256,128]{1,0:T(8,128)}, f32[256,128]{1,0:T(8,128)}, f32[256,128]{1,0:T(8,128)}, /*index=5*/f32[48,128]{1,0:T(8,128)}) custom-call(f32[256,128]{1,0:T(8,128)} %get-tuple-element.107.refs_0_, f32[256,128]{1,0:T(8,128)} %get-tuple-element.108.refs_1_, f32[256,128]{1,0:T(8,128)} %get-tuple-element.109.refs_2_, ...), custom_call_target="tpu_custom_call" | custom-call | tf_op jit(solution)/shard_map/c/pallas_call | solution.py:433
  115.4 1.9 collective-permute-start.5
  119.2 2.1 %d.4 = (f32[256,128]{1,0:T(8,128)}, f32[256,128]{1,0:T(8,128)}) custom-call(f32[256,128]{1,0:T(8,128)} %get-tuple-element.117.p, f32[256,128]{1,0:T(8,128)} %get-tuple-element.118.w, f32[256,128]{1,0:T(8,128)} %get-tuple-element.90.r.refs_4_.refs_6_, f32[48,128]{1,0:T(8,128)} %copy-done.9, f32[256,128]{1,0:T(8,128)} %get-tuple-element.92.wu, ...), custom_call_target="tpu_custom_call" | custom-call | tf_op jit(solution)/shard_map/d/pallas_call | solution.py:433
  121.4 16.3 %all_to_all.21 = f32[8,32,128]{2,1,0:T(8,128)} all-to-all(f32[8,32,128]{2,1,0:T(8,128)} %bitcast.27), channel_id=1, replica_groups=mesh['elem'=64,'lev'=8] {'lev'}, dimensions={0} | all-to-all | bytes 262144 | tf_op jit(solution)/shard_map/all_to_all | solution.py:451
  137.7 3.0 %e.3 = (f32[256,128]{1,0:T(8,128)}, f32[256,128]{1,0:T(8,128)}, f32[256,128]{1,0:T(8,128)}, f32[256,128]{1,0:T(8,128)}, f32[256,128]{1,0:T(8,128)}, /*index=5*/f32[192,128]{1,0:T(8,128)}, f32[192,128]{1,0:T(8,128)}) custom-call(f32[256,128]{1,0:T(8,128)} %get-tuple-element.120.p, f32[256,128]{1,0:T(8,128)} %get-tuple-element.118.w, ...), custom_call_target="tpu_custom_call" | custom-call | tf_op jit(solution)/shard_map/e/pallas_call | solution.py:433
  140.6 1.9 collective-permute-start.6
  144.7 2.1 %b.3 = (f32[256,128]{1,0:T(8,128)}, f32[256,128]{1,0:T(8,128)}) custom-call(f32[256,128]{1,0:T(8,128)} %get-tuple-element.125.refs_0_, f32[256,128]{1,0:T(8,128)} %get-tuple-element.126.refs_1_, f32[256,128]{1,0:T(8,128)} %get-tuple-element.127.refs_2_, f32[256,128]{1,0:T(8,128)} %get-tuple-element.128.refs_3_, ...), custom_call_target="tpu_custom_call" | custom-call | tf_op jit(solution)/shard_map/b/pallas_call | solution.py:433
  146.7 11.0 %collective-permute-start.7 = (f32[256,128]{1,0:T(8,128)}, f32[256,128]{1,0:T(8,128)S(1)}, u32[]{:S(2)}, u32[]{:S(2)}) collective-permute-start(f32[256,128]{1,0:T(8,128)} %get-tuple-element.133), channel_id=1, source_target_pairs={{0,504},{8,16},{16,8},{24,32},{32,24},{40,48},{48,40},{56,64},{64,... | collective-permute-start | bytes 393224 | tf_op jit(solution)/shard_map/ppermute | solution.py:467
  157.7 10.6 %collective-permute-done.7.refs_10_ = f32[256,128]{1,0:T(8,128)S(1)} collective-permute-done((f32[256,128]{1,0:T(8,128)}, f32[256,128]{1,0:T(8,128)S(1)}, u32[]{:S(2)}, u32[]{:S(2)}) %collective-permute-start.7) | collective-permute-done | bytes 131104 | tf_op jit(solution)/shard_map/ppermute | solution.py:467
  168.9 2.4 %c.3 = (f32[256,128]{1,0:T(8,128)}, f32[256,128]{1,0:T(8,128)}, f32[256,128]{1,0:T(8,128)}, f32[256,128]{1,0:T(8,128)}, f32[256,128]{1,0:T(8,128)}, /*index=5*/f32[48,128]{1,0:T(8,128)}) custom-call(f32[256,128]{1,0:T(8,128)} %get-tuple-element.125.refs_0_, f32[256,128]{1,0:T(8,128)} %get-tuple-element.126.refs_1_, f32[256,128]{1,0:T(8,128)} %get-tuple-element.127.refs_2_, ...), custom_call_target="tpu_custom_call" | custom-call | tf_op jit(solution)/shard_map/c/pallas_call | solution.py:433
  171.3 1.9 collective-permute-start.8
  175.2 2.1 %d.5 = (f32[256,128]{1,0:T(8,128)}, f32[256,128]{1,0:T(8,128)}) custom-call(f32[256,128]{1,0:T(8,128)} %get-tuple-element.134.p, f32[256,128]{1,0:T(8,128)} %get-tuple-element.135.w, f32[256,128]{1,0:T(8,128)} %get-tuple-element.90.r.refs_4_.refs_6_, f32[48,128]{1,0:T(8,128)} %copy-done.8, f32[256,128]{1,0:T(8,128)} %get-tuple-element.92.wu, ...), custom_call_target="tpu_custom_call" | custom-call | tf_op jit(solution)/shard_map/d/pallas_call | solution.py:433
  177.3 16.2 %all_to_all.22 = f32[8,32,128]{2,1,0:T(8,128)} all-to-all(f32[8,32,128]{2,1,0:T(8,128)} %bitcast.25), channel_id=1, replica_groups=mesh['elem'=64,'lev'=8] {'lev'}, dimensions={0} | all-to-all | bytes 262144 | tf_op jit(solution)/shard_map/all_to_all | solution.py:451
  193.5 2.8 %out.1 = (f32[256,128]{1,0:T(8,128)}, f32[256,128]{1,0:T(8,128)}, f32[256,128]{1,0:T(8,128)}, f32[256,128]{1,0:T(8,128)}, f32[256,128]{1,0:T(8,128)}) custom-call(s32[1,128]{1,0:T(1,128)} %order.5, f32[256,128]{1,0:T(8,128)} %get-tuple-element.137.p, f32[256,128]{1,0:T(8,128)} %get-tuple-element.135.w, f32[256,128]{1,0:T(8,128)} %get-tuple-element.138.g, ...), custom_call_target="tpu_custom_call" | custom-call | tf_op jit(solution)/shard_map/out/pallas_call | solution.py:433
  (26 shorter events, 12.1 us)
Async XLA Ops:
  2.9 47.0 %all-to-all-start = ((f32[8,80,128]{2,1,0:T(8,128)}), f32[8,80,128]{2,1,0:T(8,128)S(1)}, u32[]{:S(2)}, u32[]{:S(2)}) async-start(f32[8,80,128]{2,1,0:T(8,128)} %bitcast.21), calls=%async_computation | async-start | bytes 655360 | tf_op jit(solution)/shard_map/all_to_all | solution.py:451
  18.4 3.4 %collective-permute-start = (f32[240,128]{1,0:T(8,128)}, f32[240,128]{1,0:T(8,128)S(1)}, u32[]{:S(2)}, u32[]{:S(2)}) collective-permute-start(f32[240,128]{1,0:T(8,128)} %get-tuple-element.83.refs_6_), channel_id=1, source_target_pairs={{0,8},{8,0},{16,24},{24,16},{32,40},{40,32},{48,56},{56,48},{64,72... | collective-permute-start | bytes 368648 | tf_op jit(solution)/shard_map/ppermute | solution.py:462
  21.8 0.6 copy-start.4
  24.6 20.1 %collective-permute-start.1 = (f32[320,128]{1,0:T(8,128)}, f32[320,128]{1,0:T(8,128)S(1)}, u32[]{:S(2)}, u32[]{:S(2)}) collective-permute-start(f32[320,128]{1,0:T(8,128)} %get-tuple-element.87), channel_id=1, source_target_pairs={{0,504},{8,16},{16,8},{24,32},{32,24},{40,48},{48,40},{56,64},{64,... | collective-permute-start | bytes 491528 | tf_op jit(solution)/shard_map/ppermute | solution.py:467
  44.8 0.7 copy-start.1
  48.0 4.7 %collective-permute-start.2 = (f32[48,128]{1,0:T(8,128)}, f32[48,128]{1,0:T(8,128)S(1)}, u32[]{:S(2)}, u32[]{:S(2)}) collective-permute-start(f32[48,128]{1,0:T(8,128)} %get-tuple-element.91), channel_id=1, source_target_pairs={{0,8},{8,0},{16,24},{24,16},{32,40},{40,32},{48,56},{56,48},{64,72... | collective-permute-start | bytes 73736 | tf_op jit(solution)/shard_map/ppermute | solution.py:479
  49.9 0.7 copy-start
  52.7 0.6 copy-start.7
  83.5 3.4 %collective-permute-start.3 = (f32[192,128]{1,0:T(8,128)}, f32[192,128]{1,0:T(8,128)S(1)}, u32[]{:S(2)}, u32[]{:S(2)}) collective-permute-start(f32[192,128]{1,0:T(8,128)} %get-tuple-element.113.refs_5_), channel_id=1, source_target_pairs={{0,8},{8,0},{16,24},{24,16},{32,40},{40,32},{48,56},{56,48},{64,72... | collective-permute-start | bytes 294920 | tf_op jit(solution)/shard_map/ppermute | solution.py:462
  86.8 0.6 copy-start.5
  89.5 22.8 %collective-permute-start.4 = (f32[256,128]{1,0:T(8,128)}, f32[256,128]{1,0:T(8,128)S(1)}, u32[]{:S(2)}, u32[]{:S(2)}) collective-permute-start(f32[256,128]{1,0:T(8,128)} %get-tuple-element.116), channel_id=1, source_target_pairs={{0,504},{8,16},{16,8},{24,32},{32,24},{40,48},{48,40},{56,64},{64,... | collective-permute-start | bytes 393224 | tf_op jit(solution)/shard_map/ppermute | solution.py:467
  112.3 0.7 copy-start.3
  115.4 3.3 %collective-permute-start.5 = (f32[48,128]{1,0:T(8,128)}, f32[48,128]{1,0:T(8,128)S(1)}, u32[]{:S(2)}, u32[]{:S(2)}) collective-permute-start(f32[48,128]{1,0:T(8,128)} %get-tuple-element.119), channel_id=1, source_target_pairs={{0,8},{8,0},{16,24},{24,16},{32,40},{40,32},{48,56},{56,48},{64,72... | collective-permute-start | bytes 73736 | tf_op jit(solution)/shard_map/ppermute | solution.py:479
  118.6 0.6 copy-start.9
  140.6 3.4 %collective-permute-start.6 = (f32[192,128]{1,0:T(8,128)}, f32[192,128]{1,0:T(8,128)S(1)}, u32[]{:S(2)}, u32[]{:S(2)}) collective-permute-start(f32[192,128]{1,0:T(8,128)} %get-tuple-element.130.refs_5_), channel_id=1, source_target_pairs={{0,8},{8,0},{16,24},{24,16},{32,40},{40,32},{48,56},{56,48},{64,72... | collective-permute-start | bytes 294920 | tf_op jit(solution)/shard_map/ppermute | solution.py:462
  144.0 0.6 copy-start.6
  146.7 21.6 %collective-permute-start.7 = (f32[256,128]{1,0:T(8,128)}, f32[256,128]{1,0:T(8,128)S(1)}, u32[]{:S(2)}, u32[]{:S(2)}) collective-permute-start(f32[256,128]{1,0:T(8,128)} %get-tuple-element.133), channel_id=1, source_target_pairs={{0,504},{8,16},{16,8},{24,32},{32,24},{40,48},{48,40},{56,64},{64,... | collective-permute-start | bytes 393224 | tf_op jit(solution)/shard_map/ppermute | solution.py:467
  168.3 0.7 copy-start.2
  171.3 3.3 %collective-permute-start.8 = (f32[48,128]{1,0:T(8,128)}, f32[48,128]{1,0:T(8,128)S(1)}, u32[]{:S(2)}, u32[]{:S(2)}) collective-permute-start(f32[48,128]{1,0:T(8,128)} %get-tuple-element.136), channel_id=1, source_target_pairs={{0,8},{8,0},{16,24},{24,16},{32,40},{40,32},{48,56},{56,48},{64,72... | collective-permute-start | bytes 73736 | tf_op jit(solution)/shard_map/ppermute | solution.py:479
  174.6 0.6 copy-start.8
where the time goes:
time: 197 us; the launch traced here: 196 us
  starting transfers between devices  60.1 us (31%)
  blocking collectives  57.6 us (29%)
  Pallas kernels  35.8 us (18%)
  waiting for transfers between devices  35.6 us (18%)
  local copies, waits for them, and re-layouts  6.36 us (3%)
    all_to_all x3, blocking collectives, swap_levels(): lax.all_to_all(x.reshape(8, -1, LANES), 'lev', 0, 0, tiled=True)  57.6 us
    ppermute x3, starting transfers between devices, body(): rb = lax.ppermute(bm, 'elem', others)  36 us
    pallas_call x15, Pallas kernels, call(): pl.pallas_call(kernel, out_shape=[jax.ShapeDtypeStruct((n * NL, LANES), F...  35.8 us
    ppermute x3, waiting for transfers between devices, body(): rb = lax.ppermute(bm, 'elem', others)  28.4 us
    all_to_all x1, starting transfers between devices, swap_levels(): lax.all_to_all(x.reshape(8, -1, LANES), 'lev', 0, 0, tiled=True)  12.6 us
    unnamed x20, local copies, waits for them, and re-layouts  6.36 us
    ppermute x3, starting transfers between devices, body(): rd = lax.ppermute(dm, 'elem', mates)  5.73 us
    ppermute x3, starting transfers between devices, body(): ra = lax.ppermute(ta, 'elem', mates)  5.72 us
  transfers between devices with their start and end apart: 10, of which 8 were waited for; matrix products, arithmetic and copies ran while one was open for 0% of the time, Pallas kernels for 5%

commit v1 on v0

--- a/solution.py
+++ b/solution.py
@@ -428,14 +428,18 @@
     put(edge, 4, cqp)
 
 
-def call(kernel, name, args, outs, scratch=()):
+def call(kernel, name, args, outs, scratch=(), free_in=False, free_out=False):
     vmem = pl.BlockSpec(memory_space=pltpu.VMEM)
+    if not free_in:
+        args = [pltpu.with_memory_space_constraint(x, pltpu.VMEM) if x.dtype == F32 else x for x in args]
+    kind = jax.ShapeDtypeStruct if free_out else pltpu.VMEM
     return pl.pallas_call(
         kernel,
-        out_shape=[jax.ShapeDtypeStruct((n * NL, LANES), F32) for n in outs],
+        out_shape=[kind((n * NL, LANES), F32) for n in outs],
         in_specs=[vmem] * len(args),
         out_specs=[vmem] * len(outs),
         scratch_shapes=[pltpu.VMEM((n * NL, LANES), F32) for n in scratch],
+        compiler_params=pltpu.CompilerParams(vmem_limit_bytes=8 << 20),
         name=name,
     )(*args)
 
@@ -450,10 +454,10 @@
     def swap_levels(x):
         return lax.all_to_all(x.reshape(8, -1, LANES), "lev", 0, 0, tiled=True).reshape(-1, LANES)
 
-    (sent,) = call(k_col, "col", [order, flat(stiffness)], [40], [16, 16])
+    (sent,) = call(k_col, "col", [order, flat(stiffness)], [40], [16, 16], free_in=True)
     got = swap_levels(sent)
     u, v, w, g, p, m, r, ta, tb = call(
-        k_init, "init", [order, u, v, w, p, g, lm], [16] * 7 + [15, 15], [16] * 4
+        k_init, "init", [order, u, v, w, p, g, lm], [16] * 7 + [15, 15], [16] * 4, free_in=True
     )
     mn = r3 = None
     statics = None
@@ -489,7 +493,7 @@
                 k_e, "e", [p, w, g, u, v, rv] + statics + [m, r], [16] * 5 + [12, 12], [16] * 4
             )
         else:
-            outs = call(k_out, "out", [order, p, w, g, u, v, rv] + statics, [16] * 5, [16] * 2)
+            outs = call(k_out, "out", [order, p, w, g, u, v, rv] + statics, [16] * 5, [16] * 2, free_out=True)
     return tuple(x.reshape(zonal.shape) for x in outs)
 
 

time: 197 us -> 163 us (0.83)
  Pallas kernels: 35.8 us -> 6.89 us
  local copies, waits for them, and re-layouts: 6.36 us -> 1.58 us
  waiting for transfers between devices: 35.6 us -> 39.4 us
  starting transfers between devices: 60.1 us -> 56.7 us
    pallas_call x15, Pallas kernels: 35.8 us -> 6.89 us  [call(): pl.pallas_call(kernel, out_shape=[kind((n * NL, LANES), F32) for n in out...]
    unnamed x20 -> x16, local copies, waits for them, and re-layouts: 6.36 us -> 1.58 us
    ppermute x3, waiting for transfers between devices: 28.4 us -> 32.3 us  [body(): rb = lax.ppermute(bm, 'elem', others)]
    ppermute x3, starting transfers between devices: 36 us -> 32.4 us  [body(): rb = lax.ppermute(bm, 'elem', others)]
  transfers between devices with their start and end apart: 10 -> 10, of which waited for: 8 -> 9; matrix products, arithmetic and copies ran while one was open for 0% -> 0% of each run, Pallas kernels for 5% -> 1%
where the time goes in v1:
time: 163 us
  blocking collectives  57.4 us (35%)
  starting transfers between devices  56.7 us (35%)
  waiting for transfers between devices  39.4 us (24%)
  Pallas kernels  6.89 us (4%)
    all_to_all x3, blocking collectives, swap_levels(): lax.all_to_all(x.reshape(8, -1, LANES), 'lev', 0, 0, tiled=True)  57.4 us
    ppermute x3, starting transfers between devices, body(): rb = lax.ppermute(bm, 'elem', others)  32.4 us
    ppermute x3, waiting for transfers between devices, body(): rb = lax.ppermute(bm, 'elem', others)  32.3 us
    all_to_all x1, starting transfers between devices, swap_levels(): lax.all_to_all(x.reshape(8, -1, LANES), 'lev', 0, 0, tiled=True)  12.8 us
    pallas_call x15, Pallas kernels, call(): pl.pallas_call(kernel, out_shape=[kind((n * NL, LANES), F32) for n in out...  6.89 us
    ppermute x3, starting transfers between devices, body(): ra = lax.ppermute(ta, 'elem', mates)  5.76 us
    ppermute x3, starting transfers between devices, body(): rd = lax.ppermute(dm, 'elem', mates)  5.76 us
    ppermute x3, waiting for transfers between devices, body(): ra = lax.ppermute(ta, 'elem', mates)  3.84 us
  transfers between devices with their start and end apart: 10, of which 9 were waited for; matrix products, arithmetic and copies ran while one was open for 0% of the time, Pallas kernels for 1%

profile of v1, /device:TPU:32, one launch (start us, length us, event | category | flops | bytes accessed | tf_op | source)
XLA Modules:
  0.0 162.8 jit_solution(7918721147469161661)
XLA Ops:
  0.6 0.6 copy-done.7
  1.3 0.9 copy-done
  2.2 1.3 col.1
  3.5 12.8 %all-to-all-start = ((f32[8,80,128]{2,1,0:T(8,128)}), f32[8,80,128]{2,1,0:T(8,128)S(1)}, u32[]{:S(2)}, u32[]{:S(2)}) async-start(f32[8,80,128]{2,1,0:T(8,128)} %bitcast.7), calls=%async_computation | async-start | bytes 655360 | tf_op jit(solution)/shard_map/all_to_all | solution.py:455
  16.3 0.8 init.1
  17.1 1.9 %collective-permute-start = (f32[240,128]{1,0:T(8,128)S(1)}, f32[240,128]{1,0:T(8,128)S(1)}, u32[]{:S(2)}, u32[]{:S(2)}) collective-permute-start(f32[240,128]{1,0:T(8,128)S(1)} %get-tuple-element.83.refs_6_), channel_id=1, source_target_pairs={{0,8},{8,0},{16,24},{24,16},{32,40},{40,32},{48,56},{56,48},{64,72... | collective-permute-start | bytes 368648 | tf_op jit(solution)/shard_map/ppermute | solution.py:466
  19.1 1.3 collective-permute-done.refs_7_
  20.5 12.6 %collective-permute-start.1 = (f32[320,128]{1,0:T(8,128)S(1)}, f32[320,128]{1,0:T(8,128)S(1)}, u32[]{:S(2)}, u32[]{:S(2)}) collective-permute-start(f32[320,128]{1,0:T(8,128)S(1)} %get-tuple-element.87), channel_id=1, source_target_pairs={{0,504},{8,16},{16,8},{24,32},{32,24},{40,48},{48,40},{56,64},{64,... | collective-permute-start | bytes 491528 | tf_op jit(solution)/shard_map/ppermute | solution.py:471
  33.1 8.6 %collective-permute-done.1.refs_10_ = f32[320,128]{1,0:T(8,128)S(1)} collective-permute-done((f32[320,128]{1,0:T(8,128)S(1)}, f32[320,128]{1,0:T(8,128)S(1)}, u32[]{:S(2)}, u32[]{:S(2)}) %collective-permute-start.1) | collective-permute-done | bytes 163872 | tf_op jit(solution)/shard_map/ppermute | solution.py:471
  41.7 0.3 c1.1
  42.0 1.9 %collective-permute-start.2 = (f32[48,128]{1,0:T(8,128)S(1)}, f32[48,128]{1,0:T(8,128)S(1)}, u32[]{:S(2)}, u32[]{:S(2)}) collective-permute-start(f32[48,128]{1,0:T(8,128)S(1)} %get-tuple-element.91), channel_id=1, source_target_pairs={{0,8},{8,0},{16,24},{24,16},{32,40},{40,32},{48,56},{56,48},{64,72... | collective-permute-start | bytes 73736 | tf_op jit(solution)/shard_map/ppermute | solution.py:483
  44.0 0.3 stat.1
  44.2 0.9 collective-permute-done.2.rd
  45.4 25.4 %all_to_all.20 = f32[8,32,128]{2,1,0:T(8,128)S(1)} all-to-all(f32[8,32,128]{2,1,0:T(8,128)S(1)} %bitcast.25), channel_id=1, replica_groups=mesh['elem'=64,'lev'=8] {'lev'}, dimensions={0} | all-to-all | bytes 262144 | tf_op jit(solution)/shard_map/all_to_all | solution.py:455
  70.7 0.6 e.2
  71.3 1.9 %collective-permute-start.3 = (f32[192,128]{1,0:T(8,128)S(1)}, f32[192,128]{1,0:T(8,128)S(1)}, u32[]{:S(2)}, u32[]{:S(2)}) collective-permute-start(f32[192,128]{1,0:T(8,128)S(1)} %get-tuple-element.113.refs_5_), channel_id=1, source_target_pairs={{0,8},{8,0},{16,24},{24,16},{32,40},{40,32},{48,56},{56,48},{64,72... | collective-permute-start | bytes 294920 | tf_op jit(solution)/shard_map/ppermute | solution.py:466
  73.3 1.3 collective-permute-done.3.refs_6_
  74.6 10.4 %collective-permute-start.4 = (f32[256,128]{1,0:T(8,128)S(1)}, f32[256,128]{1,0:T(8,128)S(1)}, u32[]{:S(2)}, u32[]{:S(2)}) collective-permute-start(f32[256,128]{1,0:T(8,128)S(1)} %get-tuple-element.116), channel_id=1, source_target_pairs={{0,504},{8,16},{16,8},{24,32},{32,24},{40,48},{48,40},{56,64},{64,... | collective-permute-start | bytes 393224 | tf_op jit(solution)/shard_map/ppermute | solution.py:471
  85.1 10.9 %collective-permute-done.4.refs_10_ = f32[256,128]{1,0:T(8,128)S(1)} collective-permute-done((f32[256,128]{1,0:T(8,128)S(1)}, f32[256,128]{1,0:T(8,128)S(1)}, u32[]{:S(2)}, u32[]{:S(2)}) %collective-permute-start.4) | collective-permute-done | bytes 131104 | tf_op jit(solution)/shard_map/ppermute | solution.py:471
  96.2 1.9 %collective-permute-start.5 = (f32[48,128]{1,0:T(8,128)S(1)}, f32[48,128]{1,0:T(8,128)S(1)}, u32[]{:S(2)}, u32[]{:S(2)}) collective-permute-start(f32[48,128]{1,0:T(8,128)S(1)} %get-tuple-element.119), channel_id=1, source_target_pairs={{0,8},{8,0},{16,24},{24,16},{32,40},{40,32},{48,56},{56,48},{64,72... | collective-permute-start | bytes 73736 | tf_op jit(solution)/shard_map/ppermute | solution.py:483
  98.2 1.2 collective-permute-done.5.rd
  99.6 16.9 %all_to_all.21 = f32[8,32,128]{2,1,0:T(8,128)S(1)} all-to-all(f32[8,32,128]{2,1,0:T(8,128)S(1)} %bitcast.26), channel_id=1, replica_groups=mesh['elem'=64,'lev'=8] {'lev'}, dimensions={0} | all-to-all | bytes 262144 | tf_op jit(solution)/shard_map/all_to_all | solution.py:455
  116.5 0.6 e.3
  117.1 1.9 %collective-permute-start.6 = (f32[192,128]{1,0:T(8,128)S(1)}, f32[192,128]{1,0:T(8,128)S(1)}, u32[]{:S(2)}, u32[]{:S(2)}) collective-permute-start(f32[192,128]{1,0:T(8,128)S(1)} %get-tuple-element.130.refs_5_), channel_id=1, source_target_pairs={{0,8},{8,0},{16,24},{24,16},{32,40},{40,32},{48,56},{56,48},{64,72... | collective-permute-start | bytes 294920 | tf_op jit(solution)/shard_map/ppermute | solution.py:466
  119.0 1.3 collective-permute-done.6.refs_6_
  120.4 9.4 %collective-permute-start.7 = (f32[256,128]{1,0:T(8,128)S(1)}, f32[256,128]{1,0:T(8,128)S(1)}, u32[]{:S(2)}, u32[]{:S(2)}) collective-permute-start(f32[256,128]{1,0:T(8,128)S(1)} %get-tuple-element.133), channel_id=1, source_target_pairs={{0,504},{8,16},{16,8},{24,32},{32,24},{40,48},{48,40},{56,64},{64,... | collective-permute-start | bytes 393224 | tf_op jit(solution)/shard_map/ppermute | solution.py:471
  129.8 12.8 %collective-permute-done.7.refs_10_ = f32[256,128]{1,0:T(8,128)S(1)} collective-permute-done((f32[256,128]{1,0:T(8,128)S(1)}, f32[256,128]{1,0:T(8,128)S(1)}, u32[]{:S(2)}, u32[]{:S(2)}) %collective-permute-start.7) | collective-permute-done | bytes 131104 | tf_op jit(solution)/shard_map/ppermute | solution.py:471
  142.6 0.3 c.3
  142.8 1.9 %collective-permute-start.8 = (f32[48,128]{1,0:T(8,128)S(1)}, f32[48,128]{1,0:T(8,128)S(1)}, u32[]{:S(2)}, u32[]{:S(2)}) collective-permute-start(f32[48,128]{1,0:T(8,128)S(1)} %get-tuple-element.136), channel_id=1, source_target_pairs={{0,8},{8,0},{16,24},{24,16},{32,40},{40,32},{48,56},{56,48},{64,72... | collective-permute-start | bytes 73736 | tf_op jit(solution)/shard_map/ppermute | solution.py:483
  144.8 1.2 collective-permute-done.8.rd
  146.2 15.2 %all_to_all.22 = f32[8,32,128]{2,1,0:T(8,128)S(1)} all-to-all(f32[8,32,128]{2,1,0:T(8,128)S(1)} %bitcast.24), channel_id=1, replica_groups=mesh['elem'=64,'lev'=8] {'lev'}, dimensions={0} | all-to-all | bytes 262144 | tf_op jit(solution)/shard_map/all_to_all | solution.py:455
  161.3 1.4 out.1
  (22 shorter events, 1.3 us)
Async XLA Ops:
  0.6 0.7 copy-start.7
  1.3 0.9 copy-start
  2.2 14.1 %copy-start.6 = (f32[16,16,128]{2,1,0:T(8,128)S(1)}, f32[16,16,128]{2,1,0:T(8,128)}, u32[]{:S(2)}) copy-start(f32[16,16,128]{2,1,0:T(8,128)} %param.13) | copy-start | bytes 393220
  3.5 12.8 %copy-start.1 = (f32[16,16,128]{2,1,0:T(8,128)S(1)}, f32[16,16,128]{2,1,0:T(8,128)}, u32[]{:S(2)}) copy-start(f32[16,16,128]{2,1,0:T(8,128)} %param.8) | copy-start | bytes 393220
  3.5 12.8 %copy-start.2 = (f32[16,16,128]{2,1,0:T(8,128)S(1)}, f32[16,16,128]{2,1,0:T(8,128)}, u32[]{:S(2)}) copy-start(f32[16,16,128]{2,1,0:T(8,128)} %param.9) | copy-start | bytes 393220
  3.5 12.8 %copy-start.3 = (f32[16,16,128]{2,1,0:T(8,128)S(1)}, f32[16,16,128]{2,1,0:T(8,128)}, u32[]{:S(2)}) copy-start(f32[16,16,128]{2,1,0:T(8,128)} %param.10) | copy-start | bytes 393220
  3.5 12.8 %copy-start.4 = (f32[16,16,128]{2,1,0:T(8,128)S(1)}, f32[16,16,128]{2,1,0:T(8,128)}, u32[]{:S(2)}) copy-start(f32[16,16,128]{2,1,0:T(8,128)} %param.11) | copy-start | bytes 393220
  3.5 12.8 %copy-start.5 = (f32[16,16,128]{2,1,0:T(8,128)S(1)}, f32[16,16,128]{2,1,0:T(8,128)}, u32[]{:S(2)}) copy-start(f32[16,16,128]{2,1,0:T(8,128)} %param.12) | copy-start | bytes 393220
  3.5 40.4 %all-to-all-start = ((f32[8,80,128]{2,1,0:T(8,128)}), f32[8,80,128]{2,1,0:T(8,128)S(1)}, u32[]{:S(2)}, u32[]{:S(2)}) async-start(f32[8,80,128]{2,1,0:T(8,128)} %bitcast.7), calls=%async_computation | async-start | bytes 655360 | tf_op jit(solution)/shard_map/all_to_all | solution.py:455
  17.1 3.2 %collective-permute-start = (f32[240,128]{1,0:T(8,128)S(1)}, f32[240,128]{1,0:T(8,128)S(1)}, u32[]{:S(2)}, u32[]{:S(2)}) collective-permute-start(f32[240,128]{1,0:T(8,128)S(1)} %get-tuple-element.83.refs_6_), channel_id=1, source_target_pairs={{0,8},{8,0},{16,24},{24,16},{32,40},{40,32},{48,56},{56,48},{64,72... | collective-permute-start | bytes 368648 | tf_op jit(solution)/shard_map/ppermute | solution.py:466
  20.5 21.2 %collective-permute-start.1 = (f32[320,128]{1,0:T(8,128)S(1)}, f32[320,128]{1,0:T(8,128)S(1)}, u32[]{:S(2)}, u32[]{:S(2)}) collective-permute-start(f32[320,128]{1,0:T(8,128)S(1)} %get-tuple-element.87), channel_id=1, source_target_pairs={{0,504},{8,16},{16,8},{24,32},{32,24},{40,48},{48,40},{56,64},{64,... | collective-permute-start | bytes 491528 | tf_op jit(solution)/shard_map/ppermute | solution.py:471
  42.0 3.1 %collective-permute-start.2 = (f32[48,128]{1,0:T(8,128)S(1)}, f32[48,128]{1,0:T(8,128)S(1)}, u32[]{:S(2)}, u32[]{:S(2)}) collective-permute-start(f32[48,128]{1,0:T(8,128)S(1)} %get-tuple-element.91), channel_id=1, source_target_pairs={{0,8},{8,0},{16,24},{24,16},{32,40},{40,32},{48,56},{56,48},{64,72... | collective-permute-start | bytes 73736 | tf_op jit(solution)/shard_map/ppermute | solution.py:483
  71.3 3.2 %collective-permute-start.3 = (f32[192,128]{1,0:T(8,128)S(1)}, f32[192,128]{1,0:T(8,128)S(1)}, u32[]{:S(2)}, u32[]{:S(2)}) collective-permute-start(f32[192,128]{1,0:T(8,128)S(1)} %get-tuple-element.113.refs_5_), channel_id=1, source_target_pairs={{0,8},{8,0},{16,24},{24,16},{32,40},{40,32},{48,56},{56,48},{64,72... | collective-permute-start | bytes 294920 | tf_op jit(solution)/shard_map/ppermute | solution.py:466
  74.6 21.3 %collective-permute-start.4 = (f32[256,128]{1,0:T(8,128)S(1)}, f32[256,128]{1,0:T(8,128)S(1)}, u32[]{:S(2)}, u32[]{:S(2)}) collective-permute-start(f32[256,128]{1,0:T(8,128)S(1)} %get-tuple-element.116), channel_id=1, source_target_pairs={{0,504},{8,16},{16,8},{24,32},{32,24},{40,48},{48,40},{56,64},{64,... | collective-permute-start | bytes 393224 | tf_op jit(solution)/shard_map/ppermute | solution.py:471
  96.2 3.1 %collective-permute-start.5 = (f32[48,128]{1,0:T(8,128)S(1)}, f32[48,128]{1,0:T(8,128)S(1)}, u32[]{:S(2)}, u32[]{:S(2)}) collective-permute-start(f32[48,128]{1,0:T(8,128)S(1)} %get-tuple-element.119), channel_id=1, source_target_pairs={{0,8},{8,0},{16,24},{24,16},{32,40},{40,32},{48,56},{56,48},{64,72... | collective-permute-start | bytes 73736 | tf_op jit(solution)/shard_map/ppermute | solution.py:483
  117.1 3.2 %collective-permute-start.6 = (f32[192,128]{1,0:T(8,128)S(1)}, f32[192,128]{1,0:T(8,128)S(1)}, u32[]{:S(2)}, u32[]{:S(2)}) collective-permute-start(f32[192,128]{1,0:T(8,128)S(1)} %get-tuple-element.130.refs_5_), channel_id=1, source_target_pairs={{0,8},{8,0},{16,24},{24,16},{32,40},{40,32},{48,56},{56,48},{64,72... | collective-permute-start | bytes 294920 | tf_op jit(solution)/shard_map/ppermute | solution.py:466
  120.4 22.2 %collective-permute-start.7 = (f32[256,128]{1,0:T(8,128)S(1)}, f32[256,128]{1,0:T(8,128)S(1)}, u32[]{:S(2)}, u32[]{:S(2)}) collective-permute-start(f32[256,128]{1,0:T(8,128)S(1)} %get-tuple-element.133), channel_id=1, source_target_pairs={{0,504},{8,16},{16,8},{24,32},{32,24},{40,48},{48,40},{56,64},{64,... | collective-permute-start | bytes 393224 | tf_op jit(solution)/shard_map/ppermute | solution.py:471
  142.8 3.1 %collective-permute-start.8 = (f32[48,128]{1,0:T(8,128)S(1)}, f32[48,128]{1,0:T(8,128)S(1)}, u32[]{:S(2)}, u32[]{:S(2)}) collective-permute-start(f32[48,128]{1,0:T(8,128)S(1)} %get-tuple-element.136), channel_id=1, source_target_pairs={{0,8},{8,0},{16,24},{24,16},{32,40},{40,32},{48,56},{56,48},{64,72... | collective-permute-start | bytes 73736 | tf_op jit(solution)/shard_map/ppermute | solution.py:483

commit v2 on v1

--- a/solution.py
+++ b/solution.py
@@ -17,8 +17,8 @@
 F32 = jnp.float32
 LANES = 128
 NL = 16
-ROWS = 36
-PAD = 40
+ORDER = (4, 3, 5, 2, 6, 1, 7, 0)
+ROWS = 24
 
 
 def tables():
@@ -128,10 +128,23 @@
                         put(ta if i == 3 else tb, f * 3 + j - 1, row[j])
 
 
-def k_init(order, u_in, v_in, w_in, p_in, g_in, lm_in, u, v, w, g, p, m, r, ta, tb, us, vs, ws, gs):
+def fetch(sources, targets, sem):
+    copies = [pltpu.make_async_copy(a, b, sem.at[k]) for k, (a, b) in enumerate(zip(sources, targets))]
+    for copy in copies:
+        copy.start()
+    return copies
+
+
+def k_init(order, *refs):
+    ins, (u, v, w, g, p, m, r, ta, tb) = refs[:6], refs[6:15]
+    us, vs, ws, gs, order_s, sem = refs[15:19] + refs[25:]
+    held = refs[19:25]
+    copies = fetch((order,) + ins, (order_s,) + held, sem)
     core, sg = place()
-    index = jnp.broadcast_to(inverse_of(order), (NL, LANES))
-    for src, dst in ((p_in, p), (lm_in, m), (u_in, us), (v_in, vs), (w_in, ws), (g_in, gs)):
+    copies[0].wait()
+    index = jnp.broadcast_to(inverse_of(order_s), (NL, LANES))
+    for copy, src, dst in zip(copies[1:], held, (p, m, us, vs, ws, gs)):
+        copy.wait()
         for i in range(4):
             for j in range(4):
                 start = jnp.where(core == 1, (3 - i) * 4 + j, i * 4 + j)
@@ -228,7 +241,7 @@
     return ref[pl.ds((n % 2) * 8 + n // 2, NL, stride=16), :]
 
 
-def k_d(p, w, r, rd, wu, pu, wd, pd, po, vm):
+def k_d(p, w, r, rd, wu, pu, wd, pd, edge, po, vm):
     me = lax.axis_index("lev")
     got = three(rd, 0)
     for n in range(12):
@@ -243,25 +256,27 @@
         su = a if su is None else su + a
         sd = b if sd is None else sd + b
     low, high = level(po, 0), level(po, NL - 1)
-    for c in range(8):
+    su_far = su + rows(edge, 6) * high
+    sd_far = sd - rows(edge, 5) * low
+    for k, c in enumerate(ORDER):
         above = c > me
-        vm[c * 32 : c * 32 + 16, :] = jnp.where(above, su, sd)
-        vm[c * 32 + 16 : c * 32 + 32, :] = jnp.where(above, high, low)
-
-
-def solve(p, w, rv, ia, hr, rh, cp, cc, edge, s_out, p_out):
+        total = jnp.where(above, jnp.where(c > me + 1, su_far, su), jnp.where(c < me - 1, sd_far, sd))
+        vm[k * 32 : k * 32 + 16, :] = total
+        vm[k * 32 + 16 : k * 32 + 32, :] = jnp.where(above, high, low)
+
+
+def solve(p, w, rv, ia, hr, rh, cp, edge, s_out, p_out):
     me = lax.axis_index("lev")
     low, high = level(p, 0), level(p, NL - 1)
-    from_below = -rows(edge, 0) * low
-    from_above = rows(edge, 1) * high
-    for c in range(8):
-        part = rows(cc, 2 * c) * rows(rv, 2 * c) + rows(cc, 2 * c + 1) * rows(rv, 2 * c + 1)
+    from_below = from_above = prev = then = jnp.zeros_like(low)
+    for k, c in enumerate(ORDER):
+        part, side = rows(rv, 2 * k), rows(rv, 2 * k + 1)
         from_below = from_below + jnp.where(c < me, part, 0.0)
         from_above = from_above + jnp.where(c > me, part, 0.0)
-    prev = rv[pl.ds(pl.multiple_of(jnp.maximum(me - 1, 0) * 32 + 16, 16), 16), :]
-    then = rv[pl.ds(pl.multiple_of(jnp.minimum(me + 1, 7) * 32 + 16, 16), 16), :]
-    prev = jnp.where(me > 0, prev, 0.0)
-    then = jnp.where(me < 7, then, 0.0)
+        prev = jnp.where(c == me - 1, side, prev)
+        then = jnp.where(c == me + 1, side, then)
+    from_below = from_below * rows(edge, 7) - rows(edge, 0) * low
+    from_above = from_above * rows(edge, 8) + rows(edge, 1) * high
     d = []
     last = from_below
     for k in range(NL):
@@ -282,9 +297,9 @@
         after, s = s, nxt
 
 
-def k_e(p, w, g, u, v, rv, ia, hr, rh, cp, cc, edge, m, r, uo, vo, wo, go, po, ta, tb, ss, ps, ws, gs):
+def k_e(p, w, g, u, v, rv, ia, hr, rh, cp, edge, m, r, uo, vo, wo, go, po, ta, tb, ss, ps, ws, gs):
     _, sg = place()
-    solve(p, w, rv, ia, hr, rh, cp, cc, edge, ss, ps)
+    solve(p, w, rv, ia, hr, rh, cp, edge, ss, ps)
     for n in range(16):
         s = node_of(ss, n)
         put(ws, n, s)
@@ -293,9 +308,9 @@
     stage_a(sg, (u, v, ws, gs), po, m, r, (uo, vo, wo, go), ta, tb)
 
 
-def k_out(order, p, w, g, u, v, rv, ia, hr, rh, cp, cc, edge, uo, vo, wo, po, go, ss, ps):
+def k_out(order, p, w, g, u, v, rv, ia, hr, rh, cp, edge, uo, vo, wo, po, go, ss, ps):
     core, _ = place()
-    solve(p, w, rv, ia, hr, rh, cp, cc, edge, ss, ps)
+    solve(p, w, rv, ia, hr, rh, cp, edge, ss, ps)
     index = jnp.broadcast_to(order[...], (NL, LANES))
     for i in range(4):
         for j in range(4):
@@ -312,8 +327,11 @@
                 out[pl.ds(start, NL, stride=16), :] = pick(value, index)
 
 
-def k_col(order, st, out, a_s, ia_s):
-    index = jnp.broadcast_to(inverse_of(order), (NL, LANES))
+def k_col(order, st_in, out, a_s, ia_s, st, order_s, sem):
+    copies = fetch((order, st_in), (order_s, st), sem)
+    for copy in copies:
+        copy.wait()
+    index = jnp.broadcast_to(inverse_of(order_s), (NL, LANES))
     for k in range(16):
         a = pick(st[k * 16 : k * 16 + 16, :], index)
         a_s[k * 16 : k * 16 + 16, :] = a
@@ -322,61 +340,38 @@
     zero = jnp.zeros((2, LANES), F32)
     pair = lambda ref, k: ref[2 * k : 2 * k + 2, :]
     th, de = one, one
-    th_last, rho = [], [one]
+    below, rho = [one], [one]
     for k in range(128):
         de = de + th * pair(ia_s, k)
         th = th + de
         if k % 16 == 15:
-            th_last.append(th)
+            below.append(th)
             rho.append(de / th)
     ps, de = one, one
-    ps_first, sig = [None] * 8, [None] * 9
-    sig[8] = one
+    above, sig = [one] * 9, [one] * 9
     for k in range(127, -1, -1):
         de = de + ps * pair(ia_s, k)
         ps = ps + de
         if k % 16 == 0:
-            ps_first[k // 16] = ps
+            above[k // 16] = ps
             sig[k // 16] = de / ps
-    inv_th = [1.0 / x for x in th_last]
-    inv_ps = [1.0 / x for x in ps_first]
-    half = lambda k: 0.5 * jnp.sqrt(pair(ia_s, k))
-    lo_half = [half(16 * c + 16) if c < 7 else zero for c in range(8)]
-    hi_half = [half(16 * c - 1) if c > 0 else zero for c in range(8)]
-    for b in range(8):
-        def send(t, value):
-            out[b * 80 + 2 * t : b * 80 + 2 * t + 2, :] = value
-
-        for k in range(16):
-            send(k, pair(a_s, b * 16 + k))
-        for c in range(8):
-            cs = cq = zero
-            if c < b:
-                cs = th_last[c] * inv_th[b - 1]
-                if c < b - 1:
-                    cq = cs * lo_half[c]
-            elif c > b:
-                cs = ps_first[c] * inv_ps[b + 1]
-                if c > b + 1:
-                    cq = -cs * hi_half[c]
-            send(16 + 2 * c, cs)
-            send(17 + 2 * c, cq)
-        send(32, rho[b])
-        send(33, sig[b + 1])
-        send(34, hi_half[b])
-        send(35, lo_half[b])
-        for t in range(ROWS, PAD):
-            send(t, zero)
-
-
-def k_stat(got, ia, hr, rh, cp, wu, pu, wd, pd, cc, edge, scr, tu_s, td_s):
+    half = lambda k: 0.5 * jnp.sqrt(pair(ia_s, k)) if 0 <= k < 128 else zero
+    for place_of, b in enumerate(ORDER):
+        tail = [rho[b], sig[b + 1], half(16 * b - 1), half(16 * b + 16), below[b], above[b + 1], zero, zero]
+        for t in range(ROWS):
+            start = (place_of * ROWS + t) * 2
+            out[start : start + 2, :] = pair(a_s, b * 16 + t) if t < 16 else tail[t - 16]
+
+
+def k_stat(got, ia, hr, rh, cp, wu, pu, wd, pd, edge, scr, tu_s, td_s):
     core, _ = place()
-    for s in range(8):
-        src = jnp.where(core == 1, s ^ 6, s)
-        scr[s * 80 : (s + 1) * 80, :] = got[pl.ds(pl.multiple_of(src * 80, 8), 80), :]
+    size = 2 * ROWS
+    for k, src in enumerate(ORDER):
+        goal = jnp.where(core == 1, src ^ 6, src)
+        scr[pl.ds(pl.multiple_of(goal * size, 8), size), :] = got[k * size : (k + 1) * size, :]
 
     def row(t):
-        return jnp.concatenate([scr[pl.ds(2 * t + e, 8, stride=80), :] for e in range(2)], 0)
+        return jnp.concatenate([scr[pl.ds(2 * t + e, 8, stride=2 * ROWS), :] for e in range(2)], 0)
 
     for k in range(NL):
         a = row(k)
@@ -385,26 +380,19 @@
         put(ia, k, ra)
         put(rh, k, 0.5 * root)
         put(hr, k, 0.5 * (ra * root))
-    for t in range(16):
-        put(cc, t, row(16 + t))
-    rho, sig, h_lo, h_hi = row(32), row(33), row(34), row(35)
-    th, de = jnp.ones_like(rho), rho
+    rho, sig, h_lo, h_hi, th0, ps0 = (row(16 + t) for t in range(6))
+    th, de = th0, rho * th0
     for k in range(NL):
         de = de + th * rows(ia, k)
         new = th + de
         put(cp, k, th / new)
         put(tu_s, k, th)
         th = new
-    inv_th = 1.0 / th
-    ps, de = jnp.ones_like(rho), sig
+    ps, de = ps0, sig * ps0
     for k in range(NL - 1, -1, -1):
         de = de + ps * rows(ia, k)
         put(td_s, k, ps)
         ps = ps + de
-    inv_ps = 1.0 / ps
-    for ref, inv in ((tu_s, inv_th), (td_s, inv_ps)):
-        for k in range(NL):
-            put(ref, k, rows(ref, k) * inv)
     cpm, cqp = 1.0 - rho, 1.0 - sig
     for ref, wt, pt, in ((tu_s, wu, pu), (td_s, wd, pd)):
         for k in range(NL):
@@ -426,19 +414,29 @@
     put(edge, 2, 1.0 / (1.0 - rows(cp, NL - 1) * cqp))
     put(edge, 3, cpm)
     put(edge, 4, cqp)
-
-
-def call(kernel, name, args, outs, scratch=(), free_in=False, free_out=False):
+    put(edge, 5, ps * h_lo)
+    put(edge, 6, th * h_hi)
+    put(edge, 7, 1.0 / th0)
+    put(edge, 8, 1.0 / ps0)
+
+
+def call(kernel, name, args, outs, scratch=(), hbm_in=0, free_out=False):
     vmem = pl.BlockSpec(memory_space=pltpu.VMEM)
-    if not free_in:
-        args = [pltpu.with_memory_space_constraint(x, pltpu.VMEM) if x.dtype == F32 else x for x in args]
+    hbm = pl.BlockSpec(memory_space=pl.ANY)
+    args = [
+        pltpu.with_memory_space_constraint(x, pltpu.HBM if k < hbm_in else pltpu.VMEM) if k < hbm_in or x.dtype == F32 else x
+        for k, x in enumerate(args)
+    ]
     kind = jax.ShapeDtypeStruct if free_out else pltpu.VMEM
+    spare = [pltpu.VMEM((n * NL, LANES), F32) for n in scratch]
+    if hbm_in:
+        spare += [pltpu.VMEM((1, LANES), jnp.int32), pltpu.SemaphoreType.DMA((hbm_in,))]
     return pl.pallas_call(
         kernel,
         out_shape=[kind((n * NL, LANES), F32) for n in outs],
-        in_specs=[vmem] * len(args),
+        in_specs=[hbm if k < hbm_in else vmem for k in range(len(args))],
         out_specs=[vmem] * len(outs),
-        scratch_shapes=[pltpu.VMEM((n * NL, LANES), F32) for n in scratch],
+        scratch_shapes=spare,
         compiler_params=pltpu.CompilerParams(vmem_limit_bytes=8 << 20),
         name=name,
     )(*args)
@@ -452,12 +450,12 @@
     u, v, w, p, g, lm = (flat(x) for x in (zonal, meridional, vertical, pressure, geopotential, layer_mass))
 
     def swap_levels(x):
-        return lax.all_to_all(x.reshape(8, -1, LANES), "lev", 0, 0, tiled=True).reshape(-1, LANES)
-
-    (sent,) = call(k_col, "col", [order, flat(stiffness)], [40], [16, 16], free_in=True)
+        return lax.all_to_all(x.reshape(8, -1, LANES), "lev", 0, 0, tiled=True, axis_index_groups=[list(ORDER)]).reshape(-1, LANES)
+
+    (sent,) = call(k_col, "col", [order, flat(stiffness)], [ROWS], [16, 16, 16], hbm_in=2)
     got = swap_levels(sent)
     u, v, w, g, p, m, r, ta, tb = call(
-        k_init, "init", [order, u, v, w, p, g, lm], [16] * 7 + [15, 15], [16] * 4, free_in=True
+        k_init, "init", [order, p, lm, u, v, w, g], [16] * 7 + [15, 15], [16] * 10, hbm_in=7
     )
     mn = r3 = None
     statics = None
@@ -482,11 +480,11 @@
             )
         rd = lax.ppermute(dm, "elem", mates)
         if first:
-            ia, hr, rh, cp, wu, pu, wd, pd, cc, edge = call(
-                k_stat, "stat", [got], [16] * 8 + [16, 5], [40, 16, 16]
+            ia, hr, rh, cp, wu, pu, wd, pd, edge = call(
+                k_stat, "stat", [got], [16] * 8 + [9], [ROWS, 16, 16]
             )
-            statics = [ia, hr, rh, cp, cc, edge]
-        p, vm = call(k_d, "d", [p, w, r, rd, wu, pu, wd, pd], [16, 16])
+            statics = [ia, hr, rh, cp, edge]
+        p, vm = call(k_d, "d", [p, w, r, rd, wu, pu, wd, pd, edge], [16, 16])
         rv = swap_levels(vm)
         if step < SUBSTEPS - 1:
             u, v, w, g, p, ta, tb = call(

time: 163 us -> 153 us (0.939)
  blocking collectives: 57.4 us -> 45 us
  starting transfers between devices: 56.7 us -> 62.9 us
  waiting for transfers between devices: 39.4 us -> 33.6 us
  Pallas kernels: 6.89 us -> 8.84 us
    all_to_all x3, blocking collectives: 57.4 us -> 45 us  [swap_levels(): lax.all_to_all(x.reshape(8, -1, LANES), 'lev', 0, 0, tiled=True, axis_ind...]
    ppermute x3, starting transfers between devices: 32.4 us -> 39.6 us  [body(): rb = lax.ppermute(bm, 'elem', others)]
    ppermute x3, waiting for transfers between devices: 32.3 us -> 26.5 us  [body(): rb = lax.ppermute(bm, 'elem', others)]
    pallas_call x15, Pallas kernels: 6.89 us -> 8.84 us  [call(): pl.pallas_call(kernel, out_shape=[kind((n * NL, LANES), F32) for n in out...]
  transfers between devices with their start and end apart: 10 -> 10, of which waited for: 9 -> 9; matrix products, arithmetic and copies ran while one was open for 0% -> 0% of each run, Pallas kernels for 1% -> 2%
where the time goes in v2:
time: 153 us; the launch traced here: 152 us
  starting transfers between devices  62.9 us (41%)
  blocking collectives  45 us (29%)
  waiting for transfers between devices  33.6 us (22%)
  Pallas kernels  8.84 us (6%)
    all_to_all x3, blocking collectives, swap_levels(): lax.all_to_all(x.reshape(8, -1, LANES), 'lev', 0, 0, tiled=True, axis_ind...  45 us
    ppermute x3, starting transfers between devices, body(): rb = lax.ppermute(bm, 'elem', others)  39.6 us
    ppermute x3, waiting for transfers between devices, body(): rb = lax.ppermute(bm, 'elem', others)  26.5 us
    all_to_all x1, starting transfers between devices, swap_levels(): lax.all_to_all(x.reshape(8, -1, LANES), 'lev', 0, 0, tiled=True, axis_ind...  11.7 us
    pallas_call x15, Pallas kernels, call(): pl.pallas_call(kernel, out_shape=[kind((n * NL, LANES), F32) for n in out...  8.84 us
    ppermute x3, starting transfers between devices, body(): ra = lax.ppermute(ta, 'elem', mates)  5.76 us
    ppermute x3, starting transfers between devices, body(): rd = lax.ppermute(dm, 'elem', mates)  5.76 us
    ppermute x3, waiting for transfers between devices, body(): ra = lax.ppermute(ta, 'elem', mates)  3.84 us
  transfers between devices with their start and end apart: 10, of which 9 were waited for; matrix products, arithmetic and copies ran while one was open for 0% of the time, Pallas kernels for 2%

profile of v2, /device:TPU:32, one launch (start us, length us, event | category | flops | bytes accessed | tf_op | source)
XLA Modules:
  0.0 151.9 jit_solution(3243713671789142672)
XLA Ops:
  0.6 2.2 %col.1 = f32[384,128]{1,0:T(8,128)} custom-call(s32[1,128]{1,0:T(1,128)} %order.5, f32[256,128]{1,0:T(8,128)} %bitcast.27), custom_call_target="tpu_custom_call" | custom-call | tf_op jit(solution)/shard_map/col/pallas_call | solution.py:434
  2.8 11.7 %all-to-all-start = ((f32[8,48,128]{2,1,0:T(8,128)}), f32[8,48,128]{2,1,0:T(8,128)S(1)}, u32[]{:S(2)}, u32[]{:S(2)}) async-start(f32[8,48,128]{2,1,0:T(8,128)} %bitcast.7), calls=%async_computation | async-start | bytes 393216 | tf_op jit(solution)/shard_map/all_to_all | solution.py:453
  14.6 2.0 %init.1 = (f32[256,128]{1,0:T(8,128)S(1)}, f32[256,128]{1,0:T(8,128)S(1)}, f32[256,128]{1,0:T(8,128)S(1)}, f32[256,128]{1,0:T(8,128)S(1)}, f32[256,128]{1,0:T(8,...) custom-call(s32[1,128]{1,0:T(1,128)} %order.5, ...), custom_call_target="tpu_custom_call" | custom-call | tf_op jit(solution)/shard_map/init/pallas_call | solution.py:434
  16.6 1.9 %collective-permute-start = (f32[240,128]{1,0:T(8,128)S(1)}, f32[240,128]{1,0:T(8,128)S(1)}, u32[]{:S(2)}, u32[]{:S(2)}) collective-permute-start(f32[240,128]{1,0:T(8,128)S(1)} %get-tuple-element.82.refs_6_), channel_id=1, source_target_pairs={{0,8},{8,0},{16,24},{24,16},{32,40},{40,32},{48,56},{56,48},{64,72... | collective-permute-start | bytes 368648 | tf_op jit(solution)/shard_map/ppermute | solution.py:464
  18.5 1.3 collective-permute-done.refs_7_
  19.9 14.2 %collective-permute-start.1 = (f32[320,128]{1,0:T(8,128)S(1)}, f32[320,128]{1,0:T(8,128)S(1)}, u32[]{:S(2)}, u32[]{:S(2)}) collective-permute-start(f32[320,128]{1,0:T(8,128)S(1)} %get-tuple-element.86), channel_id=1, source_target_pairs={{0,504},{8,16},{16,8},{24,32},{32,24},{40,48},{48,40},{56,64},{64,... | collective-permute-start | bytes 491528 | tf_op jit(solution)/shard_map/ppermute | solution.py:469
  34.2 10.6 %collective-permute-done.1.refs_10_ = f32[320,128]{1,0:T(8,128)S(1)} collective-permute-done((f32[320,128]{1,0:T(8,128)S(1)}, f32[320,128]{1,0:T(8,128)S(1)}, u32[]{:S(2)}, u32[]{:S(2)}) %collective-permute-start.1) | collective-permute-done | bytes 163872 | tf_op jit(solution)/shard_map/ppermute | solution.py:469
  44.8 0.3 c1.1
  45.1 1.9 %collective-permute-start.2 = (f32[48,128]{1,0:T(8,128)S(1)}, f32[48,128]{1,0:T(8,128)S(1)}, u32[]{:S(2)}, u32[]{:S(2)}) collective-permute-start(f32[48,128]{1,0:T(8,128)S(1)} %get-tuple-element.90), channel_id=1, source_target_pairs={{0,8},{8,0},{16,24},{24,16},{32,40},{40,32},{48,56},{56,48},{64,72... | collective-permute-start | bytes 73736 | tf_op jit(solution)/shard_map/ppermute | solution.py:481
  47.2 1.0 collective-permute-done.2.rd
  48.4 13.2 %all_to_all.20 = f32[8,32,128]{2,1,0:T(8,128)S(1)} all-to-all(f32[8,32,128]{2,1,0:T(8,128)S(1)} %bitcast.25), channel_id=1, replica_groups={{4,3,5,2,6,1,7,0},{12,11,13,10,14,9,15,8},{20,19,21,18,22,17,23,16},{28..., dimensions={0} | all-to-all | bytes 262144 | tf_op jit(solution)/shard_map/all_to_all | solution.py:453
  61.6 0.6 e.2
  62.2 1.9 %collective-permute-start.3 = (f32[192,128]{1,0:T(8,128)S(1)}, f32[192,128]{1,0:T(8,128)S(1)}, u32[]{:S(2)}, u32[]{:S(2)}) collective-permute-start(f32[192,128]{1,0:T(8,128)S(1)} %get-tuple-element.111.refs_5_), channel_id=1, source_target_pairs={{0,8},{8,0},{16,24},{24,16},{32,40},{40,32},{48,56},{56,48},{64,72... | collective-permute-start | bytes 294920 | tf_op jit(solution)/shard_map/ppermute | solution.py:464
  64.1 1.3 collective-permute-done.3.refs_6_
  65.5 14.2 %collective-permute-start.4 = (f32[256,128]{1,0:T(8,128)S(1)}, f32[256,128]{1,0:T(8,128)S(1)}, u32[]{:S(2)}, u32[]{:S(2)}) collective-permute-start(f32[256,128]{1,0:T(8,128)S(1)} %get-tuple-element.114), channel_id=1, source_target_pairs={{0,504},{8,16},{16,8},{24,32},{32,24},{40,48},{48,40},{56,64},{64,... | collective-permute-start | bytes 393224 | tf_op jit(solution)/shard_map/ppermute | solution.py:469
  79.7 6.5 %collective-permute-done.4.refs_10_ = f32[256,128]{1,0:T(8,128)S(1)} collective-permute-done((f32[256,128]{1,0:T(8,128)S(1)}, f32[256,128]{1,0:T(8,128)S(1)}, u32[]{:S(2)}, u32[]{:S(2)}) %collective-permute-start.4) | collective-permute-done | bytes 131104 | tf_op jit(solution)/shard_map/ppermute | solution.py:469
  86.2 0.2 c.2
  86.5 1.9 %collective-permute-start.5 = (f32[48,128]{1,0:T(8,128)S(1)}, f32[48,128]{1,0:T(8,128)S(1)}, u32[]{:S(2)}, u32[]{:S(2)}) collective-permute-start(f32[48,128]{1,0:T(8,128)S(1)} %get-tuple-element.117), channel_id=1, source_target_pairs={{0,8},{8,0},{16,24},{24,16},{32,40},{40,32},{48,56},{56,48},{64,72... | collective-permute-start | bytes 73736 | tf_op jit(solution)/shard_map/ppermute | solution.py:481
  88.4 1.2 collective-permute-done.5.rd
  89.8 16.8 %all_to_all.21 = f32[8,32,128]{2,1,0:T(8,128)S(1)} all-to-all(f32[8,32,128]{2,1,0:T(8,128)S(1)} %bitcast.26), channel_id=1, replica_groups={{4,3,5,2,6,1,7,0},{12,11,13,10,14,9,15,8},{20,19,21,18,22,17,23,16},{28..., dimensions={0} | all-to-all | bytes 262144 | tf_op jit(solution)/shard_map/all_to_all | solution.py:453
  106.6 0.6 e.3
  107.2 1.9 %collective-permute-start.6 = (f32[192,128]{1,0:T(8,128)S(1)}, f32[192,128]{1,0:T(8,128)S(1)}, u32[]{:S(2)}, u32[]{:S(2)}) collective-permute-start(f32[192,128]{1,0:T(8,128)S(1)} %get-tuple-element.128.refs_5_), channel_id=1, source_target_pairs={{0,8},{8,0},{16,24},{24,16},{32,40},{40,32},{48,56},{56,48},{64,72... | collective-permute-start | bytes 294920 | tf_op jit(solution)/shard_map/ppermute | solution.py:464
  109.1 1.3 collective-permute-done.6.refs_6_
  110.5 11.2 %collective-permute-start.7 = (f32[256,128]{1,0:T(8,128)S(1)}, f32[256,128]{1,0:T(8,128)S(1)}, u32[]{:S(2)}, u32[]{:S(2)}) collective-permute-start(f32[256,128]{1,0:T(8,128)S(1)} %get-tuple-element.131), channel_id=1, source_target_pairs={{0,504},{8,16},{16,8},{24,32},{32,24},{40,48},{48,40},{56,64},{64,... | collective-permute-start | bytes 393224 | tf_op jit(solution)/shard_map/ppermute | solution.py:469
  121.7 9.4 %collective-permute-done.7.refs_10_ = f32[256,128]{1,0:T(8,128)S(1)} collective-permute-done((f32[256,128]{1,0:T(8,128)S(1)}, f32[256,128]{1,0:T(8,128)S(1)}, u32[]{:S(2)}, u32[]{:S(2)}) %collective-permute-start.7) | collective-permute-done | bytes 131104 | tf_op jit(solution)/shard_map/ppermute | solution.py:469
  131.1 0.3 c.3
  131.4 1.9 %collective-permute-start.8 = (f32[48,128]{1,0:T(8,128)S(1)}, f32[48,128]{1,0:T(8,128)S(1)}, u32[]{:S(2)}, u32[]{:S(2)}) collective-permute-start(f32[48,128]{1,0:T(8,128)S(1)} %get-tuple-element.134), channel_id=1, source_target_pairs={{0,8},{8,0},{16,24},{24,16},{32,40},{40,32},{48,56},{56,48},{64,72... | collective-permute-start | bytes 73736 | tf_op jit(solution)/shard_map/ppermute | solution.py:481
  133.3 1.2 collective-permute-done.8.rd
  134.5 0.2 d.5
  134.7 15.1 %all_to_all.22 = f32[8,32,128]{2,1,0:T(8,128)S(1)} all-to-all(f32[8,32,128]{2,1,0:T(8,128)S(1)} %bitcast.24), channel_id=1, replica_groups={{4,3,5,2,6,1,7,0},{12,11,13,10,14,9,15,8},{20,19,21,18,22,17,23,16},{28..., dimensions={0} | all-to-all | bytes 262144 | tf_op jit(solution)/shard_map/all_to_all | solution.py:453
  149.8 0.7 copy-done
  150.5 1.4 out.1
  (8 shorter events, 0.9 us)
Async XLA Ops:
  2.8 44.2 %all-to-all-start = ((f32[8,48,128]{2,1,0:T(8,128)}), f32[8,48,128]{2,1,0:T(8,128)S(1)}, u32[]{:S(2)}, u32[]{:S(2)}) async-start(f32[8,48,128]{2,1,0:T(8,128)} %bitcast.7), calls=%async_computation | async-start | bytes 393216 | tf_op jit(solution)/shard_map/all_to_all | solution.py:453
  16.6 3.2 %collective-permute-start = (f32[240,128]{1,0:T(8,128)S(1)}, f32[240,128]{1,0:T(8,128)S(1)}, u32[]{:S(2)}, u32[]{:S(2)}) collective-permute-start(f32[240,128]{1,0:T(8,128)S(1)} %get-tuple-element.82.refs_6_), channel_id=1, source_target_pairs={{0,8},{8,0},{16,24},{24,16},{32,40},{40,32},{48,56},{56,48},{64,72... | collective-permute-start | bytes 368648 | tf_op jit(solution)/shard_map/ppermute | solution.py:464
  19.9 24.8 %collective-permute-start.1 = (f32[320,128]{1,0:T(8,128)S(1)}, f32[320,128]{1,0:T(8,128)S(1)}, u32[]{:S(2)}, u32[]{:S(2)}) collective-permute-start(f32[320,128]{1,0:T(8,128)S(1)} %get-tuple-element.86), channel_id=1, source_target_pairs={{0,504},{8,16},{16,8},{24,32},{32,24},{40,48},{48,40},{56,64},{64,... | collective-permute-start | bytes 491528 | tf_op jit(solution)/shard_map/ppermute | solution.py:469
  45.1 3.1 %collective-permute-start.2 = (f32[48,128]{1,0:T(8,128)S(1)}, f32[48,128]{1,0:T(8,128)S(1)}, u32[]{:S(2)}, u32[]{:S(2)}) collective-permute-start(f32[48,128]{1,0:T(8,128)S(1)} %get-tuple-element.90), channel_id=1, source_target_pairs={{0,8},{8,0},{16,24},{24,16},{32,40},{40,32},{48,56},{56,48},{64,72... | collective-permute-start | bytes 73736 | tf_op jit(solution)/shard_map/ppermute | solution.py:481
  62.2 3.2 %collective-permute-start.3 = (f32[192,128]{1,0:T(8,128)S(1)}, f32[192,128]{1,0:T(8,128)S(1)}, u32[]{:S(2)}, u32[]{:S(2)}) collective-permute-start(f32[192,128]{1,0:T(8,128)S(1)} %get-tuple-element.111.refs_5_), channel_id=1, source_target_pairs={{0,8},{8,0},{16,24},{24,16},{32,40},{40,32},{48,56},{56,48},{64,72... | collective-permute-start | bytes 294920 | tf_op jit(solution)/shard_map/ppermute | solution.py:464
  65.5 20.7 %collective-permute-start.4 = (f32[256,128]{1,0:T(8,128)S(1)}, f32[256,128]{1,0:T(8,128)S(1)}, u32[]{:S(2)}, u32[]{:S(2)}) collective-permute-start(f32[256,128]{1,0:T(8,128)S(1)} %get-tuple-element.114), channel_id=1, source_target_pairs={{0,504},{8,16},{16,8},{24,32},{32,24},{40,48},{48,40},{56,64},{64,... | collective-permute-start | bytes 393224 | tf_op jit(solution)/shard_map/ppermute | solution.py:469
  86.5 3.1 %collective-permute-start.5 = (f32[48,128]{1,0:T(8,128)S(1)}, f32[48,128]{1,0:T(8,128)S(1)}, u32[]{:S(2)}, u32[]{:S(2)}) collective-permute-start(f32[48,128]{1,0:T(8,128)S(1)} %get-tuple-element.117), channel_id=1, source_target_pairs={{0,8},{8,0},{16,24},{24,16},{32,40},{40,32},{48,56},{56,48},{64,72... | collective-permute-start | bytes 73736 | tf_op jit(solution)/shard_map/ppermute | solution.py:481
  107.2 3.2 %collective-permute-start.6 = (f32[192,128]{1,0:T(8,128)S(1)}, f32[192,128]{1,0:T(8,128)S(1)}, u32[]{:S(2)}, u32[]{:S(2)}) collective-permute-start(f32[192,128]{1,0:T(8,128)S(1)} %get-tuple-element.128.refs_5_), channel_id=1, source_target_pairs={{0,8},{8,0},{16,24},{24,16},{32,40},{40,32},{48,56},{56,48},{64,72... | collective-permute-start | bytes 294920 | tf_op jit(solution)/shard_map/ppermute | solution.py:464
  110.5 20.6 %collective-permute-start.7 = (f32[256,128]{1,0:T(8,128)S(1)}, f32[256,128]{1,0:T(8,128)S(1)}, u32[]{:S(2)}, u32[]{:S(2)}) collective-permute-start(f32[256,128]{1,0:T(8,128)S(1)} %get-tuple-element.131), channel_id=1, source_target_pairs={{0,504},{8,16},{16,8},{24,32},{32,24},{40,48},{48,40},{56,64},{64,... | collective-permute-start | bytes 393224 | tf_op jit(solution)/shard_map/ppermute | solution.py:469
  131.4 3.1 %collective-permute-start.8 = (f32[48,128]{1,0:T(8,128)S(1)}, f32[48,128]{1,0:T(8,128)S(1)}, u32[]{:S(2)}, u32[]{:S(2)}) collective-permute-start(f32[48,128]{1,0:T(8,128)S(1)} %get-tuple-element.134), channel_id=1, source_target_pairs={{0,8},{8,0},{16,24},{24,16},{32,40},{40,32},{48,56},{56,48},{64,72... | collective-permute-start | bytes 73736 | tf_op jit(solution)/shard_map/ppermute | solution.py:481
  149.8 0.7 copy-start

commit v3 on v2

--- a/solution.py
+++ b/solution.py
@@ -17,7 +17,8 @@
 F32 = jnp.float32
 LANES = 128
 NL = 16
-ORDER = (4, 3, 5, 2, 6, 1, 7, 0)
+ORDER = (4, 0, 7, 1, 6, 2, 5, 3)
+LONG = 64
 ROWS = 24
 
 
@@ -308,26 +309,35 @@
     stage_a(sg, (u, v, ws, gs), po, m, r, (uo, vo, wo, go), ta, tb)
 
 
-def k_out(order, p, w, g, u, v, rv, ia, hr, rh, cp, edge, uo, vo, wo, po, go, ss, ps):
+def k_out(order, p, w, g, u, v, rv, ia, hr, rh, cp, edge, uo, vo, wo, po, go, ss, ps, us, vs, ws, qs, gs, order_s, sem):
     core, _ = place()
+    (copy,) = fetch((order,), (order_s,), sem)
+    copy.wait()
+    index = jnp.broadcast_to(order_s[...], (NL, LANES))
+
+    def store(value_of, held, out, k):
+        for n in range(16):
+            start = jnp.where(core == 1, (3 - n // 4) * 4 + n % 4, n)
+            held[pl.ds(start, NL, stride=16), :] = pick(value_of(n), index)
+        copy = pltpu.make_async_copy(held, out, sem.at[k])
+        copy.start()
+        return copy
+
+    copies = [
+        store(functools.partial(rows, u), us, uo, 1),
+        store(functools.partial(rows, v), vs, vo, 2),
+    ]
     solve(p, w, rv, ia, hr, rh, cp, edge, ss, ps)
-    index = jnp.broadcast_to(order[...], (NL, LANES))
-    for i in range(4):
-        for j in range(4):
-            n = i * 4 + j
-            start = jnp.where(core == 1, (3 - i) * 4 + j, n)
-            s = node_of(ss, n)
-            for out, value in (
-                (uo, rows(u, n)),
-                (vo, rows(v, n)),
-                (wo, s),
-                (po, node_of(ps, n)),
-                (go, rows(g, n) + RATE * s),
-            ):
-                out[pl.ds(start, NL, stride=16), :] = pick(value, index)
-
-
-def k_col(order, st_in, out, a_s, ia_s, st, order_s, sem):
+    copies += [
+        store(functools.partial(node_of, ss), ws, wo, 3),
+        store(functools.partial(node_of, ps), qs, po, 4),
+        store(lambda n: rows(g, n) + RATE * node_of(ss, n), gs, go, 5),
+    ]
+    for copy in copies:
+        copy.wait()
+
+
+def k_col(order, st_in, after, out, a_s, ia_s, st, order_s, sem):
     copies = fetch((order, st_in), (order_s, st), sem)
     for copy in copies:
         copy.wait()
@@ -363,7 +373,7 @@
             out[start : start + 2, :] = pair(a_s, b * 16 + t) if t < 16 else tail[t - 16]
 
 
-def k_stat(got, ia, hr, rh, cp, wu, pu, wd, pd, edge, scr, tu_s, td_s):
+def k_stat(got, after, ia, hr, rh, cp, wu, pu, wd, pd, edge, scr, tu_s, td_s):
     core, _ = place()
     size = 2 * ROWS
     for k, src in enumerate(ORDER):
@@ -430,12 +440,12 @@
     kind = jax.ShapeDtypeStruct if free_out else pltpu.VMEM
     spare = [pltpu.VMEM((n * NL, LANES), F32) for n in scratch]
     if hbm_in:
-        spare += [pltpu.VMEM((1, LANES), jnp.int32), pltpu.SemaphoreType.DMA((hbm_in,))]
+        spare += [pltpu.VMEM((1, LANES), jnp.int32), pltpu.SemaphoreType.DMA((8,))]
     return pl.pallas_call(
         kernel,
         out_shape=[kind((n * NL, LANES), F32) for n in outs],
         in_specs=[hbm if k < hbm_in else vmem for k in range(len(args))],
-        out_specs=[vmem] * len(outs),
+        out_specs=[hbm if free_out else vmem] * len(outs),
         scratch_shapes=spare,
         compiler_params=pltpu.CompilerParams(vmem_limit_bytes=8 << 20),
         name=name,
@@ -452,8 +462,6 @@
     def swap_levels(x):
         return lax.all_to_all(x.reshape(8, -1, LANES), "lev", 0, 0, tiled=True, axis_index_groups=[list(ORDER)]).reshape(-1, LANES)
 
-    (sent,) = call(k_col, "col", [order, flat(stiffness)], [ROWS], [16, 16, 16], hbm_in=2)
-    got = swap_levels(sent)
     u, v, w, g, p, m, r, ta, tb = call(
         k_init, "init", [order, p, lm, u, v, w, g], [16] * 7 + [15, 15], [16] * 10, hbm_in=7
     )
@@ -468,11 +476,14 @@
             f3, bm = call(functools.partial(k_b, False), "b", [u, v, w, g, r, ta, ra, tb], [16, 16])
         rb = lax.ppermute(bm, "elem", others)
         if first:
+            (sent,) = call(k_col, "col", [order, flat(stiffness), bm], [ROWS], [16, 16, 16], hbm_in=2)
+            got = swap_levels(sent)
+        if first:
             u, v, w, g, p, dm, r, mn = call(
                 functools.partial(k_c, True),
                 "c1",
                 [u, v, w, g, p, m, r, r3, f3, tb, rb],
-                [16] * 5 + [3, 16, 4],
+                [16] * 5 + [LONG, 16, 4],
             )
         else:
             u, v, w, g, p, dm = call(
@@ -481,7 +492,7 @@
         rd = lax.ppermute(dm, "elem", mates)
         if first:
             ia, hr, rh, cp, wu, pu, wd, pd, edge = call(
-                k_stat, "stat", [got], [16] * 8 + [9], [ROWS, 16, 16]
+                k_stat, "stat", [got, rd], [16] * 8 + [9], [ROWS, 16, 16]
             )
             statics = [ia, hr, rh, cp, edge]
         p, vm = call(k_d, "d", [p, w, r, rd, wu, pu, wd, pd, edge], [16, 16])
@@ -491,7 +502,7 @@
                 k_e, "e", [p, w, g, u, v, rv] + statics + [m, r], [16] * 5 + [12, 12], [16] * 4
             )
         else:
-            outs = call(k_out, "out", [order, p, w, g, u, v, rv] + statics, [16] * 5, [16] * 2, free_out=True)
+            outs = call(k_out, "out", [order, p, w, g, u, v, rv] + statics, [16] * 5, [16] * 7, hbm_in=1, free_out=True)
     return tuple(x.reshape(zonal.shape) for x in outs)
 
 

time: 153 us -> 144 us (0.941)
  waiting for transfers between devices: 33.6 us -> 22.7 us
  starting transfers between devices: 62.9 us -> 66.7 us
    ppermute x3, waiting for transfers between devices: 26.5 us -> 12.4 us  [body(): rb = lax.ppermute(bm, 'elem', others)]
    ppermute x3, starting transfers between devices: 39.6 us -> 48.4 us  [body(): rb = lax.ppermute(bm, 'elem', others)]
    all_to_all x1, starting transfers between devices: 11.7 us -> 6.76 us  [swap_levels(): lax.all_to_all(x.reshape(8, -1, LANES), 'lev', 0, 0, tiled=True, axis_ind...]
    all_to_all x1, waiting for transfers between devices: 0.01 us -> 2.31 us  [swap_levels(): lax.all_to_all(x.reshape(8, -1, LANES), 'lev', 0, 0, tiled=True, axis_ind...]
  transfers between devices with their start and end apart: 10 -> 10, of which waited for: 9 -> 10; matrix products, arithmetic and copies ran while one was open for 0% -> 0% of each run, Pallas kernels for 2% -> 2%
where the time goes in v3:
time: 144 us; the launch traced here: 143 us
  starting transfers between devices  66.7 us (46%)
  blocking collectives  43.6 us (30%)
  waiting for transfers between devices  22.7 us (16%)
  Pallas kernels  9.64 us (7%)
    ppermute x3, starting transfers between devices, body(): rb = lax.ppermute(bm, 'elem', others)  48.4 us
    all_to_all x3, blocking collectives, swap_levels(): lax.all_to_all(x.reshape(8, -1, LANES), 'lev', 0, 0, tiled=True, axis_ind...  43.6 us
    ppermute x3, waiting for transfers between devices, body(): rb = lax.ppermute(bm, 'elem', others)  12.4 us
    pallas_call x15, Pallas kernels, call(): pl.pallas_call(kernel, out_shape=[kind((n * NL, LANES), F32) for n in out...  9.64 us
    all_to_all x1, starting transfers between devices, swap_levels(): lax.all_to_all(x.reshape(8, -1, LANES), 'lev', 0, 0, tiled=True, axis_ind...  6.76 us
    ppermute x3, starting transfers between devices, body(): ra = lax.ppermute(ta, 'elem', mates)  5.76 us
    ppermute x3, starting transfers between devices, body(): rd = lax.ppermute(dm, 'elem', mates)  5.76 us
    ppermute x3, waiting for transfers between devices, body(): rd = lax.ppermute(dm, 'elem', mates)  4.2 us
  transfers between devices with their start and end apart: 10, of which 10 were waited for; matrix products, arithmetic and copies ran while one was open for 0% of the time, Pallas kernels for 2%

profile of v3, /device:TPU:32, one launch (start us, length us, event | category | flops | bytes accessed | tf_op | source)
XLA Modules:
  0.0 143.5 jit_solution(4418821887874574593)
XLA Ops:
  0.6 2.0 %init.1 = (f32[256,128]{1,0:T(8,128)S(1)}, f32[256,128]{1,0:T(8,128)S(1)}, f32[256,128]{1,0:T(8,128)S(1)}, f32[256,128]{1,0:T(8,128)S(1)}, f32[256,128]{1,0:T(8,...) custom-call(s32[1,128]{1,0:T(1,128)} %order.5, ...), custom_call_target="tpu_custom_call" | custom-call | tf_op jit(solution)/shard_map/init/pallas_call | solution.py:444
  2.7 1.9 %collective-permute-start = (f32[240,128]{1,0:T(8,128)S(1)}, f32[240,128]{1,0:T(8,128)S(1)}, u32[]{:S(2)}, u32[]{:S(2)}) collective-permute-start(f32[240,128]{1,0:T(8,128)S(1)} %get-tuple-element.82.refs_6_), channel_id=1, source_target_pairs={{0,8},{8,0},{16,24},{24,16},{32,40},{40,32},{48,56},{56,48},{64,72... | collective-permute-start | bytes 368648 | tf_op jit(solution)/shard_map/ppermute | solution.py:472
  4.6 1.3 collective-permute-done.refs_7_
  6.0 19.2 %collective-permute-start.1 = (f32[320,128]{1,0:T(8,128)S(1)}, f32[320,128]{1,0:T(8,128)S(1)}, u32[]{:S(2)}, u32[]{:S(2)}) collective-permute-start(f32[320,128]{1,0:T(8,128)S(1)} %get-tuple-element.86.after), channel_id=1, source_target_pairs={{0,504},{8,16},{16,8},{24,32},{32,24},{40,48},{48,40},{56,64},{64,... | collective-permute-start | bytes 491528 | tf_op jit(solution)/shard_map/ppermute | solution.py:477
  25.2 2.3 %col.1 = f32[384,128]{1,0:T(8,128)} custom-call(s32[1,128]{1,0:T(1,128)} %order.5, f32[256,128]{1,0:T(8,128)} %bitcast.27, f32[320,128]{1,0:T(8,128)S(1)} %get-tuple-element.86.after), custom_call_target="tpu_custom_call" | custom-call | tf_op jit(solution)/shard_map/col/pallas_call | solution.py:444
  27.5 6.8 %all-to-all-start = ((f32[8,48,128]{2,1,0:T(8,128)}), f32[8,48,128]{2,1,0:T(8,128)S(1)}, u32[]{:S(2)}, u32[]{:S(2)}) async-start(f32[8,48,128]{2,1,0:T(8,128)} %bitcast.7), calls=%async_computation | async-start | bytes 393216 | tf_op jit(solution)/shard_map/all_to_all | solution.py:463
  34.4 0.3 c1.1
  34.7 1.9 %collective-permute-start.2 = (f32[1024,128]{1,0:T(8,128)S(1)}, f32[1024,128]{1,0:T(8,128)S(1)}, u32[]{:S(2)}, u32[]{:S(2)}) collective-permute-start(f32[1024,128]{1,0:T(8,128)S(1)} %get-tuple-element.90), channel_id=1, source_target_pairs={{0,8},{8,0},{16,24},{24,16},{32,40},{40,32},{48,56},{56,48},{64,72... | collective-permute-start | bytes 1572872 | tf_op jit(solution)/shard_map/ppermute | solution.py:492
  36.7 1.9 %collective-permute-done.2.after.rd = f32[1024,128]{1,0:T(8,128)S(1)} collective-permute-done((f32[1024,128]{1,0:T(8,128)S(1)}, f32[1024,128]{1,0:T(8,128)S(1)}, u32[]{:S(2)}, u32[]{:S(2)}) %collective-permute-start.2) | collective-permute-done | bytes 524320 | tf_op jit(solution)/shard_map/ppermute | solution.py:492
  38.5 2.3 %all-to-all-done = f32[8,48,128]{2,1,0:T(8,128)S(1)} async-done(((f32[8,48,128]{2,1,0:T(8,128)}), f32[8,48,128]{2,1,0:T(8,128)S(1)}, u32[]{:S(2)}, u32[]{:S(2)}) %all-to-all-start) | async-done | bytes 196640 | tf_op jit(solution)/shard_map/all_to_all | solution.py:463
  41.0 0.3 d.3
  41.3 13.2 %all_to_all.20 = f32[8,32,128]{2,1,0:T(8,128)S(1)} all-to-all(f32[8,32,128]{2,1,0:T(8,128)S(1)} %bitcast.25), channel_id=1, replica_groups={{4,0,7,1,6,2,5,3},{12,8,15,9,14,10,13,11},{20,16,23,17,22,18,21,19},{28..., dimensions={0} | all-to-all | bytes 262144 | tf_op jit(solution)/shard_map/all_to_all | solution.py:463
  54.5 0.6 e.2
  55.1 1.9 %collective-permute-start.3 = (f32[192,128]{1,0:T(8,128)S(1)}, f32[192,128]{1,0:T(8,128)S(1)}, u32[]{:S(2)}, u32[]{:S(2)}) collective-permute-start(f32[192,128]{1,0:T(8,128)S(1)} %get-tuple-element.111.refs_5_), channel_id=1, source_target_pairs={{0,8},{8,0},{16,24},{24,16},{32,40},{40,32},{48,56},{56,48},{64,72... | collective-permute-start | bytes 294920 | tf_op jit(solution)/shard_map/ppermute | solution.py:472
  57.1 1.3 collective-permute-done.3.refs_6_
  58.4 14.5 %collective-permute-start.4 = (f32[256,128]{1,0:T(8,128)S(1)}, f32[256,128]{1,0:T(8,128)S(1)}, u32[]{:S(2)}, u32[]{:S(2)}) collective-permute-start(f32[256,128]{1,0:T(8,128)S(1)} %get-tuple-element.114), channel_id=1, source_target_pairs={{0,504},{8,16},{16,8},{24,32},{32,24},{40,48},{48,40},{56,64},{64,... | collective-permute-start | bytes 393224 | tf_op jit(solution)/shard_map/ppermute | solution.py:477
  73.0 6.1 %collective-permute-done.4.refs_10_ = f32[256,128]{1,0:T(8,128)S(1)} collective-permute-done((f32[256,128]{1,0:T(8,128)S(1)}, f32[256,128]{1,0:T(8,128)S(1)}, u32[]{:S(2)}, u32[]{:S(2)}) %collective-permute-start.4) | collective-permute-done | bytes 131104 | tf_op jit(solution)/shard_map/ppermute | solution.py:477
  79.1 0.3 c.2
  79.3 1.9 %collective-permute-start.5 = (f32[48,128]{1,0:T(8,128)S(1)}, f32[48,128]{1,0:T(8,128)S(1)}, u32[]{:S(2)}, u32[]{:S(2)}) collective-permute-start(f32[48,128]{1,0:T(8,128)S(1)} %get-tuple-element.117), channel_id=1, source_target_pairs={{0,8},{8,0},{16,24},{24,16},{32,40},{40,32},{48,56},{56,48},{64,72... | collective-permute-start | bytes 73736 | tf_op jit(solution)/shard_map/ppermute | solution.py:492
  81.3 1.2 collective-permute-done.5.rd
  82.4 0.2 d.4
  82.7 14.8 %all_to_all.21 = f32[8,32,128]{2,1,0:T(8,128)S(1)} all-to-all(f32[8,32,128]{2,1,0:T(8,128)S(1)} %bitcast.26), channel_id=1, replica_groups={{4,0,7,1,6,2,5,3},{12,8,15,9,14,10,13,11},{20,16,23,17,22,18,21,19},{28..., dimensions={0} | all-to-all | bytes 262144 | tf_op jit(solution)/shard_map/all_to_all | solution.py:463
  97.5 0.6 e.3
  98.1 1.9 %collective-permute-start.6 = (f32[192,128]{1,0:T(8,128)S(1)}, f32[192,128]{1,0:T(8,128)S(1)}, u32[]{:S(2)}, u32[]{:S(2)}) collective-permute-start(f32[192,128]{1,0:T(8,128)S(1)} %get-tuple-element.128.refs_5_), channel_id=1, source_target_pairs={{0,8},{8,0},{16,24},{24,16},{32,40},{40,32},{48,56},{56,48},{64,72... | collective-permute-start | bytes 294920 | tf_op jit(solution)/shard_map/ppermute | solution.py:472
  100.0 1.3 collective-permute-done.6.refs_6_
  101.4 14.7 %collective-permute-start.7 = (f32[256,128]{1,0:T(8,128)S(1)}, f32[256,128]{1,0:T(8,128)S(1)}, u32[]{:S(2)}, u32[]{:S(2)}) collective-permute-start(f32[256,128]{1,0:T(8,128)S(1)} %get-tuple-element.131), channel_id=1, source_target_pairs={{0,504},{8,16},{16,8},{24,32},{32,24},{40,48},{48,40},{56,64},{64,... | collective-permute-start | bytes 393224 | tf_op jit(solution)/shard_map/ppermute | solution.py:477
  116.1 6.1 %collective-permute-done.7.refs_10_ = f32[256,128]{1,0:T(8,128)S(1)} collective-permute-done((f32[256,128]{1,0:T(8,128)S(1)}, f32[256,128]{1,0:T(8,128)S(1)}, u32[]{:S(2)}, u32[]{:S(2)}) %collective-permute-start.7) | collective-permute-done | bytes 131104 | tf_op jit(solution)/shard_map/ppermute | solution.py:477
  122.2 0.3 c.3
  122.5 1.9 %collective-permute-start.8 = (f32[48,128]{1,0:T(8,128)S(1)}, f32[48,128]{1,0:T(8,128)S(1)}, u32[]{:S(2)}, u32[]{:S(2)}) collective-permute-start(f32[48,128]{1,0:T(8,128)S(1)} %get-tuple-element.134), channel_id=1, source_target_pairs={{0,8},{8,0},{16,24},{24,16},{32,40},{40,32},{48,56},{56,48},{64,72... | collective-permute-start | bytes 73736 | tf_op jit(solution)/shard_map/ppermute | solution.py:492
  124.4 1.2 collective-permute-done.8.rd
  125.8 15.6 %all_to_all.22 = f32[8,32,128]{2,1,0:T(8,128)S(1)} all-to-all(f32[8,32,128]{2,1,0:T(8,128)S(1)} %bitcast.24), channel_id=1, replica_groups={{4,0,7,1,6,2,5,3},{12,8,15,9,14,10,13,11},{20,16,23,17,22,18,21,19},{28..., dimensions={0} | all-to-all | bytes 262144 | tf_op jit(solution)/shard_map/all_to_all | solution.py:463
  141.4 2.1 %out.1 = (f32[256,128]{1,0:T(8,128)}, f32[256,128]{1,0:T(8,128)}, f32[256,128]{1,0:T(8,128)}, f32[256,128]{1,0:T(8,128)}, f32[256,128]{1,0:T(8,128)}) custom-call(s32[1,128]{1,0:T(1,128)} %order.5, f32[256,128]{1,0:T(8,128)S(1)} %get-tuple-element.135.p, f32[256,128]{1,0:T(8,128)S(1)} %get-tuple-element.133.w, f32[256,128]{1,0:T(8,128)S(1)} %get-tuple-element.136.g, ...), custom_call_target="tpu_custom_call" | custom-call | tf_op jit(solution)/shard_map/out/pallas_call | solution.py:444
  (6 shorter events, 0.9 us)
Async XLA Ops:
  2.7 3.2 %collective-permute-start = (f32[240,128]{1,0:T(8,128)S(1)}, f32[240,128]{1,0:T(8,128)S(1)}, u32[]{:S(2)}, u32[]{:S(2)}) collective-permute-start(f32[240,128]{1,0:T(8,128)S(1)} %get-tuple-element.82.refs_6_), channel_id=1, source_target_pairs={{0,8},{8,0},{16,24},{24,16},{32,40},{40,32},{48,56},{56,48},{64,72... | collective-permute-start | bytes 368648 | tf_op jit(solution)/shard_map/ppermute | solution.py:472
  6.0 28.4 %collective-permute-start.1 = (f32[320,128]{1,0:T(8,128)S(1)}, f32[320,128]{1,0:T(8,128)S(1)}, u32[]{:S(2)}, u32[]{:S(2)}) collective-permute-start(f32[320,128]{1,0:T(8,128)S(1)} %get-tuple-element.86.after), channel_id=1, source_target_pairs={{0,504},{8,16},{16,8},{24,32},{32,24},{40,48},{48,40},{56,64},{64,... | collective-permute-start | bytes 491528 | tf_op jit(solution)/shard_map/ppermute | solution.py:477
  27.5 13.4 %all-to-all-start = ((f32[8,48,128]{2,1,0:T(8,128)}), f32[8,48,128]{2,1,0:T(8,128)S(1)}, u32[]{:S(2)}, u32[]{:S(2)}) async-start(f32[8,48,128]{2,1,0:T(8,128)} %bitcast.7), calls=%async_computation | async-start | bytes 393216 | tf_op jit(solution)/shard_map/all_to_all | solution.py:463
  34.7 3.8 %collective-permute-start.2 = (f32[1024,128]{1,0:T(8,128)S(1)}, f32[1024,128]{1,0:T(8,128)S(1)}, u32[]{:S(2)}, u32[]{:S(2)}) collective-permute-start(f32[1024,128]{1,0:T(8,128)S(1)} %get-tuple-element.90), channel_id=1, source_target_pairs={{0,8},{8,0},{16,24},{24,16},{32,40},{40,32},{48,56},{56,48},{64,72... | collective-permute-start | bytes 1572872 | tf_op jit(solution)/shard_map/ppermute | solution.py:492
  55.1 3.2 %collective-permute-start.3 = (f32[192,128]{1,0:T(8,128)S(1)}, f32[192,128]{1,0:T(8,128)S(1)}, u32[]{:S(2)}, u32[]{:S(2)}) collective-permute-start(f32[192,128]{1,0:T(8,128)S(1)} %get-tuple-element.111.refs_5_), channel_id=1, source_target_pairs={{0,8},{8,0},{16,24},{24,16},{32,40},{40,32},{48,56},{56,48},{64,72... | collective-permute-start | bytes 294920 | tf_op jit(solution)/shard_map/ppermute | solution.py:472
  58.4 20.6 %collective-permute-start.4 = (f32[256,128]{1,0:T(8,128)S(1)}, f32[256,128]{1,0:T(8,128)S(1)}, u32[]{:S(2)}, u32[]{:S(2)}) collective-permute-start(f32[256,128]{1,0:T(8,128)S(1)} %get-tuple-element.114), channel_id=1, source_target_pairs={{0,504},{8,16},{16,8},{24,32},{32,24},{40,48},{48,40},{56,64},{64,... | collective-permute-start | bytes 393224 | tf_op jit(solution)/shard_map/ppermute | solution.py:477
  79.3 3.1 %collective-permute-start.5 = (f32[48,128]{1,0:T(8,128)S(1)}, f32[48,128]{1,0:T(8,128)S(1)}, u32[]{:S(2)}, u32[]{:S(2)}) collective-permute-start(f32[48,128]{1,0:T(8,128)S(1)} %get-tuple-element.117), channel_id=1, source_target_pairs={{0,8},{8,0},{16,24},{24,16},{32,40},{40,32},{48,56},{56,48},{64,72... | collective-permute-start | bytes 73736 | tf_op jit(solution)/shard_map/ppermute | solution.py:492
  98.1 3.2 %collective-permute-start.6 = (f32[192,128]{1,0:T(8,128)S(1)}, f32[192,128]{1,0:T(8,128)S(1)}, u32[]{:S(2)}, u32[]{:S(2)}) collective-permute-start(f32[192,128]{1,0:T(8,128)S(1)} %get-tuple-element.128.refs_5_), channel_id=1, source_target_pairs={{0,8},{8,0},{16,24},{24,16},{32,40},{40,32},{48,56},{56,48},{64,72... | collective-permute-start | bytes 294920 | tf_op jit(solution)/shard_map/ppermute | solution.py:472
  101.4 20.8 %collective-permute-start.7 = (f32[256,128]{1,0:T(8,128)S(1)}, f32[256,128]{1,0:T(8,128)S(1)}, u32[]{:S(2)}, u32[]{:S(2)}) collective-permute-start(f32[256,128]{1,0:T(8,128)S(1)} %get-tuple-element.131), channel_id=1, source_target_pairs={{0,504},{8,16},{16,8},{24,32},{32,24},{40,48},{48,40},{56,64},{64,... | collective-permute-start | bytes 393224 | tf_op jit(solution)/shard_map/ppermute | solution.py:477
  122.5 3.1 %collective-permute-start.8 = (f32[48,128]{1,0:T(8,128)S(1)}, f32[48,128]{1,0:T(8,128)S(1)}, u32[]{:S(2)}, u32[]{:S(2)}) collective-permute-start(f32[48,128]{1,0:T(8,128)S(1)} %get-tuple-element.134), channel_id=1, source_target_pairs={{0,8},{8,0},{16,24},{24,16},{32,40},{40,32},{48,56},{56,48},{64,72... | collective-permute-start | bytes 73736 | tf_op jit(solution)/shard_map/ppermute | solution.py:492

commit v4 on v3

--- a/solution.py
+++ b/solution.py
@@ -18,7 +18,7 @@
 LANES = 128
 NL = 16
 ORDER = (4, 0, 7, 1, 6, 2, 5, 3)
-LONG = 64
+LONG = 72
 ROWS = 24
 
 
@@ -137,14 +137,16 @@
 
 
 def k_init(order, *refs):
-    ins, (u, v, w, g, p, m, r, ta, tb) = refs[:6], refs[6:15]
-    us, vs, ws, gs, order_s, sem = refs[15:19] + refs[25:]
-    held = refs[19:25]
-    copies = fetch((order,) + ins, (order_s,) + held, sem)
+    ins, (u, v, w, g, p, m, r, ta, tb, st, index_out) = refs[:7], refs[7:18]
+    us, vs, ws, gs, order_s, sem = refs[18:22] + refs[28:]
+    held = refs[22:28]
+    copies = fetch((order,) + ins, (order_s,) + held + (st,), sem)
     core, sg = place()
     copies[0].wait()
-    index = jnp.broadcast_to(inverse_of(order_s), (NL, LANES))
-    for copy, src, dst in zip(copies[1:], held, (p, m, us, vs, ws, gs)):
+    inverse = inverse_of(order_s)
+    index_out[...] = inverse
+    index = jnp.broadcast_to(inverse, (NL, LANES))
+    for copy, src, dst in zip(copies[1:7], held, (p, m, us, vs, ws, gs)):
         copy.wait()
         for i in range(4):
             for j in range(4):
@@ -163,6 +165,7 @@
                 if j > 0:
                     put(ta if i == 3 else tb, 12 + j - 1, row[j])
     stage_a(sg, (us, vs, ws, gs), p, m, r, (u, v, w, g), ta, tb)
+    copies[7].wait()
 
 
 def k_b(first, *refs):
@@ -173,32 +176,36 @@
             put(r3, j, 1.0 / (own[j] + got[j]))
         rr = lambda j: rows(r3, j)
     else:
-        u, v, w, g, r, ta, ra, tb, f3, bm = refs
+        u, v, w, g, m, r, ta, ra, tb, f3, bm = refs
         rr = lambda j: rows(r, 12 + j)
     _, sg = place()
     for f, field in enumerate((u, v, w, g)):
         own, got = three(ta, f * 3), three(ra, f * 3)
         for j in range(4):
             put(f3, f * 4 + j, rows(field, 12 + j) + rr(j) * (own[j] + got[j]))
+    known = []
     for j in range(4):
         along = lin(D[0], [rows(u, j), rows(u, 4 + j), rows(u, 8 + j), rows(f3, j)])
         across = dy(functools.partial(rows, v), 0, j)
-        put(bm, 12 + j, sg * along + across)
+        known.append(rows(m, j) * (sg * along + across))
+    known = sew(known)
+    for j in range(1, 4):
+        put(bm, 11 + j, known[j])
     for k in range(12):
         put(bm, k, rows(tb, k))
     if first:
         for j in range(4):
-            put(bm, 16 + j, rows(m, j))
+            put(bm, 15 + j, rows(m, j))
 
 
 def k_c(first, *refs):
     if first:
         u, v, w, g, p, m, r, r3, f3, tb, rb, uo, vo, wo, go, po, dm, ro, mo = refs
-        own, got = three(tb, 12), sew([rows(rb, 16 + j) for j in range(4)])
+        own, got = three(tb, 12), sew([rows(rb, 15 + j) for j in range(4)])
         for j in range(4):
             put(ro, j, 1.0 / (own[j] + got[j]))
             put(ro, 12 + j, rows(r3, j))
-            put(mo, j, rows(rb, 16 + j))
+            put(mo, j, rows(rb, 15 + j))
             for i in (1, 2):
                 put(ro, i * 4 + j, rows(r, i * 4 + j))
         r, mn = ro, mo
@@ -220,9 +227,8 @@
             inc.append(part)
     other = []
     for j in range(4):
-        t = rows(rb, 12 + j) - (sg * D[0][0]) * inc[0][j] + lin(D[j], inc[1])
-        other.append(rows(mn, j) * (-SPEED * t))
-    other = sew(other)
+        other.append(rows(mn, j) * (lin(D[j], inc[1]) - (sg * D[0][0]) * inc[0][j]))
+    other = [-SPEED * (a + b) for a, b in zip(sew(other), three(rb, 12))]
     gu, gv = functools.partial(rows, uo), functools.partial(rows, vo)
     for i in range(4):
         row = sew([rows(m, i * 4 + j) * (-SPEED * (sg * dx(gu, i, j) + dy(gv, i, j))) for j in range(4)])
@@ -337,11 +343,8 @@
         copy.wait()
 
 
-def k_col(order, st_in, after, out, a_s, ia_s, st, order_s, sem):
-    copies = fetch((order, st_in), (order_s, st), sem)
-    for copy in copies:
-        copy.wait()
-    index = jnp.broadcast_to(inverse_of(order_s), (NL, LANES))
+def k_col(after, st, index, out, a_s, ia_s):
+    index = jnp.broadcast_to(index[...], (NL, LANES))
     for k in range(16):
         a = pick(st[k * 16 : k * 16 + 16, :], index)
         a_s[k * 16 : k * 16 + 16, :] = a
@@ -434,7 +437,7 @@
     vmem = pl.BlockSpec(memory_space=pltpu.VMEM)
     hbm = pl.BlockSpec(memory_space=pl.ANY)
     args = [
-        pltpu.with_memory_space_constraint(x, pltpu.HBM if k < hbm_in else pltpu.VMEM) if k < hbm_in or x.dtype == F32 else x
+        pltpu.with_memory_space_constraint(x, pltpu.HBM if k < hbm_in else pltpu.VMEM)
         for k, x in enumerate(args)
     ]
     kind = jax.ShapeDtypeStruct if free_out else pltpu.VMEM
@@ -443,7 +446,7 @@
         spare += [pltpu.VMEM((1, LANES), jnp.int32), pltpu.SemaphoreType.DMA((8,))]
     return pl.pallas_call(
         kernel,
-        out_shape=[kind((n * NL, LANES), F32) for n in outs],
+        out_shape=[kind((n * NL, LANES), F32) if n else kind((1, LANES), jnp.int32) for n in outs],
         in_specs=[hbm if k < hbm_in else vmem for k in range(len(args))],
         out_specs=[hbm if free_out else vmem] * len(outs),
         scratch_shapes=spare,
@@ -462,8 +465,8 @@
     def swap_levels(x):
         return lax.all_to_all(x.reshape(8, -1, LANES), "lev", 0, 0, tiled=True, axis_index_groups=[list(ORDER)]).reshape(-1, LANES)
 
-    u, v, w, g, p, m, r, ta, tb = call(
-        k_init, "init", [order, p, lm, u, v, w, g], [16] * 7 + [15, 15], [16] * 10, hbm_in=7
+    u, v, w, g, p, m, r, ta, tb, st, index = call(
+        k_init, "init", [order, p, lm, u, v, w, g, flat(stiffness)], [16] * 7 + [15, 15, 16, 0], [16] * 10, hbm_in=8
     )
     mn = r3 = None
     statics = None
@@ -471,12 +474,12 @@
         first = step == 0
         ra = lax.ppermute(ta, "elem", mates)
         if first:
-            f3, bm, r3 = call(functools.partial(k_b, True), "b1", [u, v, w, g, m, r, ta, ra, tb], [16, 20, 4])
+            f3, bm, r3 = call(functools.partial(k_b, True), "b1", [u, v, w, g, m, r, ta, ra, tb], [16, 19, 4])
         else:
-            f3, bm = call(functools.partial(k_b, False), "b", [u, v, w, g, r, ta, ra, tb], [16, 16])
+            f3, bm = call(functools.partial(k_b, False), "b", [u, v, w, g, m, r, ta, ra, tb], [16, 15])
         rb = lax.ppermute(bm, "elem", others)
         if first:
-            (sent,) = call(k_col, "col", [order, flat(stiffness), bm], [ROWS], [16, 16, 16], hbm_in=2)
+            (sent,) = call(k_col, "col", [bm, st, index], [ROWS], [16, 16])
             got = swap_levels(sent)
         if first:
             u, v, w, g, p, dm, r, mn = call(

time: 144 us -> 142 us (0.986)
    all_to_all x1, waiting for transfers between devices: 2.31 us -> 4.33 us  [swap_levels(): lax.all_to_all(x.reshape(8, -1, LANES), 'lev', 0, 0, tiled=True, axis_ind...]
    ppermute x3, waiting for transfers between devices: 4.2 us -> 2.32 us  [body(): rd = lax.ppermute(dm, 'elem', mates)]
  transfers between devices with their start and end apart: 10 -> 10, of which waited for: 10 -> 8; matrix products, arithmetic and copies ran while one was open for 0% -> 0% of each run, Pallas kernels for 2% -> 1%
where the time goes in v4:
time: 142 us
  starting transfers between devices  66.9 us (47%)
  blocking collectives  43.5 us (31%)
  waiting for transfers between devices  21.9 us (15%)
  Pallas kernels  8.71 us (6%)
    ppermute x3, starting transfers between devices, body(): rb = lax.ppermute(bm, 'elem', others)  48.6 us
    all_to_all x3, blocking collectives, swap_levels(): lax.all_to_all(x.reshape(8, -1, LANES), 'lev', 0, 0, tiled=True, axis_ind...  43.5 us
    ppermute x3, waiting for transfers between devices, body(): rb = lax.ppermute(bm, 'elem', others)  11.4 us
    pallas_call x15, Pallas kernels, call(): pl.pallas_call(kernel, out_shape=[kind((n * NL, LANES), F32) if n else ki...  8.71 us
    all_to_all x1, starting transfers between devices, swap_levels(): lax.all_to_all(x.reshape(8, -1, LANES), 'lev', 0, 0, tiled=True, axis_ind...  6.75 us
    ppermute x3, starting transfers between devices, body(): ra = lax.ppermute(ta, 'elem', mates)  5.76 us
    ppermute x3, starting transfers between devices, body(): rd = lax.ppermute(dm, 'elem', mates)  5.76 us
    all_to_all x1, waiting for transfers between devices, swap_levels(): lax.all_to_all(x.reshape(8, -1, LANES), 'lev', 0, 0, tiled=True, axis_ind...  4.33 us
  transfers between devices with their start and end apart: 10, of which 8 were waited for; matrix products, arithmetic and copies ran while one was open for 0% of the time, Pallas kernels for 1%

profile of v4, /device:TPU:32, one launch (start us, length us, event | category | flops | bytes accessed | tf_op | source)
XLA Modules:
  0.0 141.7 jit_solution(3458060841432364671)
XLA Ops:
  0.6 2.1 %init.1 = (f32[256,128]{1,0:T(8,128)S(1)}, f32[256,128]{1,0:T(8,128)S(1)}, f32[256,128]{1,0:T(8,128)S(1)}, f32[256,128]{1,0:T(8,128)S(1)}, f32[256,128]{1,0:T(8,...) custom-call(s32[1,128]{1,0:T(1,128)} %order.3, ...), custom_call_target="tpu_custom_call" | custom-call | tf_op jit(solution)/shard_map/init/pallas_call | solution.py:447
  2.7 1.9 %collective-permute-start = (f32[240,128]{1,0:T(8,128)S(1)}, f32[240,128]{1,0:T(8,128)S(1)}, u32[]{:S(2)}, u32[]{:S(2)}) collective-permute-start(f32[240,128]{1,0:T(8,128)S(1)} %get-tuple-element.84.refs_6_), channel_id=1, source_target_pairs={{0,8},{8,0},{16,24},{24,16},{32,40},{40,32},{48,56},{56,48},{64,72... | collective-permute-start | bytes 368648 | tf_op jit(solution)/shard_map/ppermute | solution.py:475
  4.6 1.3 collective-permute-done.refs_7_
  6.1 19.2 %collective-permute-start.1 = (f32[304,128]{1,0:T(8,128)S(1)}, f32[304,128]{1,0:T(8,128)S(1)}, u32[]{:S(2)}, u32[]{:S(2)}) collective-permute-start(f32[304,128]{1,0:T(8,128)S(1)} %get-tuple-element.88.after), channel_id=1, source_target_pairs={{0,504},{8,16},{16,8},{24,32},{32,24},{40,48},{48,40},{56,64},{64,... | collective-permute-start | bytes 466952 | tf_op jit(solution)/shard_map/ppermute | solution.py:480
  25.3 1.1 col.1
  26.4 6.8 %all-to-all-start = ((f32[8,48,128]{2,1,0:T(8,128)}), f32[8,48,128]{2,1,0:T(8,128)S(1)}, u32[]{:S(2)}, u32[]{:S(2)}) async-start(f32[8,48,128]{2,1,0:T(8,128)} %bitcast.7), calls=%async_computation | async-start | bytes 393216 | tf_op jit(solution)/shard_map/all_to_all | solution.py:466
  33.2 0.3 c1.1
  33.5 1.9 %collective-permute-start.2 = (f32[1152,128]{1,0:T(8,128)S(1)}, f32[1152,128]{1,0:T(8,128)S(1)}, u32[]{:S(2)}, u32[]{:S(2)}) collective-permute-start(f32[1152,128]{1,0:T(8,128)S(1)} %get-tuple-element.92), channel_id=1, source_target_pairs={{0,8},{8,0},{16,24},{24,16},{32,40},{40,32},{48,56},{56,48},{64,72... | collective-permute-start | bytes 1769480 | tf_op jit(solution)/shard_map/ppermute | solution.py:495
  35.5 4.3 %all-to-all-done = f32[8,48,128]{2,1,0:T(8,128)S(1)} async-done(((f32[8,48,128]{2,1,0:T(8,128)}), f32[8,48,128]{2,1,0:T(8,128)S(1)}, u32[]{:S(2)}, u32[]{:S(2)}) %all-to-all-start) | async-done | bytes 196640 | tf_op jit(solution)/shard_map/all_to_all | solution.py:466
  40.0 0.2 d.3
  40.2 13.1 %all_to_all.20 = f32[8,32,128]{2,1,0:T(8,128)S(1)} all-to-all(f32[8,32,128]{2,1,0:T(8,128)S(1)} %bitcast.25), channel_id=1, replica_groups={{4,0,7,1,6,2,5,3},{12,8,15,9,14,10,13,11},{20,16,23,17,22,18,21,19},{28..., dimensions={0} | all-to-all | bytes 262144 | tf_op jit(solution)/shard_map/all_to_all | solution.py:466
  53.3 0.6 e.2
  53.9 1.9 %collective-permute-start.3 = (f32[192,128]{1,0:T(8,128)S(1)}, f32[192,128]{1,0:T(8,128)S(1)}, u32[]{:S(2)}, u32[]{:S(2)}) collective-permute-start(f32[192,128]{1,0:T(8,128)S(1)} %get-tuple-element.115.refs_6_), channel_id=1, source_target_pairs={{0,8},{8,0},{16,24},{24,16},{32,40},{40,32},{48,56},{56,48},{64,72... | collective-permute-start | bytes 294920 | tf_op jit(solution)/shard_map/ppermute | solution.py:475
  55.9 1.3 collective-permute-done.3.refs_7_
  57.3 14.6 %collective-permute-start.4 = (f32[240,128]{1,0:T(8,128)S(1)}, f32[240,128]{1,0:T(8,128)S(1)}, u32[]{:S(2)}, u32[]{:S(2)}) collective-permute-start(f32[240,128]{1,0:T(8,128)S(1)} %get-tuple-element.118), channel_id=1, source_target_pairs={{0,504},{8,16},{16,8},{24,32},{32,24},{40,48},{48,40},{56,64},{64,... | collective-permute-start | bytes 368648 | tf_op jit(solution)/shard_map/ppermute | solution.py:480
  71.9 5.6 %collective-permute-done.4.refs_10_ = f32[240,128]{1,0:T(8,128)S(1)} collective-permute-done((f32[240,128]{1,0:T(8,128)S(1)}, f32[240,128]{1,0:T(8,128)S(1)}, u32[]{:S(2)}, u32[]{:S(2)}) %collective-permute-start.4) | collective-permute-done | bytes 122912 | tf_op jit(solution)/shard_map/ppermute | solution.py:480
  77.6 0.3 c.2
  77.8 1.9 %collective-permute-start.5 = (f32[48,128]{1,0:T(8,128)S(1)}, f32[48,128]{1,0:T(8,128)S(1)}, u32[]{:S(2)}, u32[]{:S(2)}) collective-permute-start(f32[48,128]{1,0:T(8,128)S(1)} %get-tuple-element.121), channel_id=1, source_target_pairs={{0,8},{8,0},{16,24},{24,16},{32,40},{40,32},{48,56},{56,48},{64,72... | collective-permute-start | bytes 73736 | tf_op jit(solution)/shard_map/ppermute | solution.py:495
  79.7 1.2 collective-permute-done.5.rd
  80.9 0.2 d.4
  81.2 14.8 %all_to_all.21 = f32[8,32,128]{2,1,0:T(8,128)S(1)} all-to-all(f32[8,32,128]{2,1,0:T(8,128)S(1)} %bitcast.26), channel_id=1, replica_groups={{4,0,7,1,6,2,5,3},{12,8,15,9,14,10,13,11},{20,16,23,17,22,18,21,19},{28..., dimensions={0} | all-to-all | bytes 262144 | tf_op jit(solution)/shard_map/all_to_all | solution.py:466
  96.0 0.6 e.3
  96.6 1.9 %collective-permute-start.6 = (f32[192,128]{1,0:T(8,128)S(1)}, f32[192,128]{1,0:T(8,128)S(1)}, u32[]{:S(2)}, u32[]{:S(2)}) collective-permute-start(f32[192,128]{1,0:T(8,128)S(1)} %get-tuple-element.132.refs_6_), channel_id=1, source_target_pairs={{0,8},{8,0},{16,24},{24,16},{32,40},{40,32},{48,56},{56,48},{64,72... | collective-permute-start | bytes 294920 | tf_op jit(solution)/shard_map/ppermute | solution.py:475
  98.6 1.3 collective-permute-done.6.refs_7_
  100.0 14.8 %collective-permute-start.7 = (f32[240,128]{1,0:T(8,128)S(1)}, f32[240,128]{1,0:T(8,128)S(1)}, u32[]{:S(2)}, u32[]{:S(2)}) collective-permute-start(f32[240,128]{1,0:T(8,128)S(1)} %get-tuple-element.135), channel_id=1, source_target_pairs={{0,504},{8,16},{16,8},{24,32},{32,24},{40,48},{48,40},{56,64},{64,... | collective-permute-start | bytes 368648 | tf_op jit(solution)/shard_map/ppermute | solution.py:480
  114.8 5.7 %collective-permute-done.7.refs_10_ = f32[240,128]{1,0:T(8,128)S(1)} collective-permute-done((f32[240,128]{1,0:T(8,128)S(1)}, f32[240,128]{1,0:T(8,128)S(1)}, u32[]{:S(2)}, u32[]{:S(2)}) %collective-permute-start.7) | collective-permute-done | bytes 122912 | tf_op jit(solution)/shard_map/ppermute | solution.py:480
  120.5 0.2 c.3
  120.8 1.9 %collective-permute-start.8 = (f32[48,128]{1,0:T(8,128)S(1)}, f32[48,128]{1,0:T(8,128)S(1)}, u32[]{:S(2)}, u32[]{:S(2)}) collective-permute-start(f32[48,128]{1,0:T(8,128)S(1)} %get-tuple-element.138), channel_id=1, source_target_pairs={{0,8},{8,0},{16,24},{24,16},{32,40},{40,32},{48,56},{56,48},{64,72... | collective-permute-start | bytes 73736 | tf_op jit(solution)/shard_map/ppermute | solution.py:495
  122.7 1.2 collective-permute-done.8.rd
  123.9 0.3 d.5
  124.1 15.5 %all_to_all.22 = f32[8,32,128]{2,1,0:T(8,128)S(1)} all-to-all(f32[8,32,128]{2,1,0:T(8,128)S(1)} %bitcast.24), channel_id=1, replica_groups={{4,0,7,1,6,2,5,3},{12,8,15,9,14,10,13,11},{20,16,23,17,22,18,21,19},{28..., dimensions={0} | all-to-all | bytes 262144 | tf_op jit(solution)/shard_map/all_to_all | solution.py:466
  139.6 2.1 %out.1 = (f32[256,128]{1,0:T(8,128)}, f32[256,128]{1,0:T(8,128)}, f32[256,128]{1,0:T(8,128)}, f32[256,128]{1,0:T(8,128)}, f32[256,128]{1,0:T(8,128)}) custom-call(s32[1,128]{1,0:T(1,128)} %order.3, f32[256,128]{1,0:T(8,128)S(1)} %get-tuple-element.139.p, f32[256,128]{1,0:T(8,128)S(1)} %get-tuple-element.137.w, f32[256,128]{1,0:T(8,128)S(1)} %get-tuple-element.140.g, ...), custom_call_target="tpu_custom_call" | custom-call | tf_op jit(solution)/shard_map/out/pallas_call | solution.py:447
  (6 shorter events, 0.6 us)
Async XLA Ops:
  2.7 3.2 %collective-permute-start = (f32[240,128]{1,0:T(8,128)S(1)}, f32[240,128]{1,0:T(8,128)S(1)}, u32[]{:S(2)}, u32[]{:S(2)}) collective-permute-start(f32[240,128]{1,0:T(8,128)S(1)} %get-tuple-element.84.refs_6_), channel_id=1, source_target_pairs={{0,8},{8,0},{16,24},{24,16},{32,40},{40,32},{48,56},{56,48},{64,72... | collective-permute-start | bytes 368648 | tf_op jit(solution)/shard_map/ppermute | solution.py:475
  6.1 27.1 %collective-permute-start.1 = (f32[304,128]{1,0:T(8,128)S(1)}, f32[304,128]{1,0:T(8,128)S(1)}, u32[]{:S(2)}, u32[]{:S(2)}) collective-permute-start(f32[304,128]{1,0:T(8,128)S(1)} %get-tuple-element.88.after), channel_id=1, source_target_pairs={{0,504},{8,16},{16,8},{24,32},{32,24},{40,48},{48,40},{56,64},{64,... | collective-permute-start | bytes 466952 | tf_op jit(solution)/shard_map/ppermute | solution.py:480
  26.4 13.3 %all-to-all-start = ((f32[8,48,128]{2,1,0:T(8,128)}), f32[8,48,128]{2,1,0:T(8,128)S(1)}, u32[]{:S(2)}, u32[]{:S(2)}) async-start(f32[8,48,128]{2,1,0:T(8,128)} %bitcast.7), calls=%async_computation | async-start | bytes 393216 | tf_op jit(solution)/shard_map/all_to_all | solution.py:466
  33.5 6.3 %collective-permute-start.2 = (f32[1152,128]{1,0:T(8,128)S(1)}, f32[1152,128]{1,0:T(8,128)S(1)}, u32[]{:S(2)}, u32[]{:S(2)}) collective-permute-start(f32[1152,128]{1,0:T(8,128)S(1)} %get-tuple-element.92), channel_id=1, source_target_pairs={{0,8},{8,0},{16,24},{24,16},{32,40},{40,32},{48,56},{56,48},{64,72... | collective-permute-start | bytes 1769480 | tf_op jit(solution)/shard_map/ppermute | solution.py:495
  53.9 3.2 %collective-permute-start.3 = (f32[192,128]{1,0:T(8,128)S(1)}, f32[192,128]{1,0:T(8,128)S(1)}, u32[]{:S(2)}, u32[]{:S(2)}) collective-permute-start(f32[192,128]{1,0:T(8,128)S(1)} %get-tuple-element.115.refs_6_), channel_id=1, source_target_pairs={{0,8},{8,0},{16,24},{24,16},{32,40},{40,32},{48,56},{56,48},{64,72... | collective-permute-start | bytes 294920 | tf_op jit(solution)/shard_map/ppermute | solution.py:475
  57.3 20.3 %collective-permute-start.4 = (f32[240,128]{1,0:T(8,128)S(1)}, f32[240,128]{1,0:T(8,128)S(1)}, u32[]{:S(2)}, u32[]{:S(2)}) collective-permute-start(f32[240,128]{1,0:T(8,128)S(1)} %get-tuple-element.118), channel_id=1, source_target_pairs={{0,504},{8,16},{16,8},{24,32},{32,24},{40,48},{48,40},{56,64},{64,... | collective-permute-start | bytes 368648 | tf_op jit(solution)/shard_map/ppermute | solution.py:480
  77.8 3.1 %collective-permute-start.5 = (f32[48,128]{1,0:T(8,128)S(1)}, f32[48,128]{1,0:T(8,128)S(1)}, u32[]{:S(2)}, u32[]{:S(2)}) collective-permute-start(f32[48,128]{1,0:T(8,128)S(1)} %get-tuple-element.121), channel_id=1, source_target_pairs={{0,8},{8,0},{16,24},{24,16},{32,40},{40,32},{48,56},{56,48},{64,72... | collective-permute-start | bytes 73736 | tf_op jit(solution)/shard_map/ppermute | solution.py:495
  96.6 3.2 %collective-permute-start.6 = (f32[192,128]{1,0:T(8,128)S(1)}, f32[192,128]{1,0:T(8,128)S(1)}, u32[]{:S(2)}, u32[]{:S(2)}) collective-permute-start(f32[192,128]{1,0:T(8,128)S(1)} %get-tuple-element.132.refs_6_), channel_id=1, source_target_pairs={{0,8},{8,0},{16,24},{24,16},{32,40},{40,32},{48,56},{56,48},{64,72... | collective-permute-start | bytes 294920 | tf_op jit(solution)/shard_map/ppermute | solution.py:475
  100.0 20.5 %collective-permute-start.7 = (f32[240,128]{1,0:T(8,128)S(1)}, f32[240,128]{1,0:T(8,128)S(1)}, u32[]{:S(2)}, u32[]{:S(2)}) collective-permute-start(f32[240,128]{1,0:T(8,128)S(1)} %get-tuple-element.135), channel_id=1, source_target_pairs={{0,504},{8,16},{16,8},{24,32},{32,24},{40,48},{48,40},{56,64},{64,... | collective-permute-start | bytes 368648 | tf_op jit(solution)/shard_map/ppermute | solution.py:480
  120.8 3.1 %collective-permute-start.8 = (f32[48,128]{1,0:T(8,128)S(1)}, f32[48,128]{1,0:T(8,128)S(1)}, u32[]{:S(2)}, u32[]{:S(2)}) collective-permute-start(f32[48,128]{1,0:T(8,128)S(1)} %get-tuple-element.138), channel_id=1, source_target_pairs={{0,8},{8,0},{16,24},{24,16},{32,40},{40,32},{48,56},{56,48},{64,72... | collective-permute-start | bytes 73736 | tf_op jit(solution)/shard_map/ppermute | solution.py:495

commit v5 on v4

--- a/solution.py
+++ b/solution.py
@@ -101,13 +101,13 @@
     return jnp.take_along_axis(values, index, axis=1, mode="promise_in_bounds")
 
 
-def stage_a(sg, src, p, m, r, dst, ta, tb):
+def stage_a(sg, src, p, m, r, dst, ta, tb, own_face):
     for f in range(4):
         if f < 2:
             get = functools.partial(rows, p)
         else:
             get = functools.partial(rows, src[f])
-        for i in range(4):
+        for i in (3,) if own_face else (0, 1, 2):
             row = []
             for j in range(4):
                 if f == 0:
@@ -123,10 +123,11 @@
                 own = rows(src[f], n)
                 if i in (1, 2):
                     put(dst[f], n, own + rows(r, n) * row[j])
-                else:
+                elif j > 0:
+                    put(ta if i == 3 else tb, f * 3 + j - 1, row[j])
+                if i == 0:
                     put(dst[f], n, own)
-                    if j > 0:
-                        put(ta if i == 3 else tb, f * 3 + j - 1, row[j])
+                    put(dst[f], 12 + j, rows(src[f], 12 + j))
 
 
 def fetch(sources, targets, sem):
@@ -137,9 +138,9 @@
 
 
 def k_init(order, *refs):
-    ins, (u, v, w, g, p, m, r, ta, tb, st, index_out) = refs[:7], refs[7:18]
-    us, vs, ws, gs, order_s, sem = refs[18:22] + refs[28:]
-    held = refs[22:28]
+    ins, (us, vs, ws, gs, p, m, r, ta, st, index_out) = refs[:7], refs[7:17]
+    order_s, sem = refs[23:]
+    held = refs[17:23]
     copies = fetch((order,) + ins, (order_s,) + held + (st,), sem)
     core, sg = place()
     copies[0].wait()
@@ -162,10 +163,18 @@
                 put(r, i * 4 + j, 1.0 / row[j])
             else:
                 put(r, i * 4 + j, row[j])
-                if j > 0:
-                    put(ta if i == 3 else tb, 12 + j - 1, row[j])
-    stage_a(sg, (us, vs, ws, gs), p, m, r, (u, v, w, g), ta, tb)
+                if i == 3 and j > 0:
+                    put(ta, 12 + j - 1, row[j])
+    stage_a(sg, (us, vs, ws, gs), p, m, r, None, ta, None, True)
     copies[7].wait()
+
+
+def k_rest(first, us, vs, ws, gs, p, m, r, u, v, w, g, tb):
+    _, sg = place()
+    stage_a(sg, (us, vs, ws, gs), p, m, r, (u, v, w, g), None, tb, False)
+    if first:
+        for j in range(1, 4):
+            put(tb, 11 + j, rows(r, j))
 
 
 def k_b(first, *refs):
@@ -304,7 +313,7 @@
         after, s = s, nxt
 
 
-def k_e(p, w, g, u, v, rv, ia, hr, rh, cp, edge, m, r, uo, vo, wo, go, po, ta, tb, ss, ps, ws, gs):
+def k_e(p, w, g, u, v, rv, ia, hr, rh, cp, edge, m, r, ws, gs, po, ta, ss, ps):
     _, sg = place()
     solve(p, w, rv, ia, hr, rh, cp, edge, ss, ps)
     for n in range(16):
@@ -312,7 +321,7 @@
         put(ws, n, s)
         put(gs, n, rows(g, n) + RATE * s)
         put(po, n, node_of(ps, n))
-    stage_a(sg, (u, v, ws, gs), po, m, r, (uo, vo, wo, go), ta, tb)
+    stage_a(sg, (u, v, ws, gs), po, m, r, None, ta, None, True)
 
 
 def k_out(order, p, w, g, u, v, rv, ia, hr, rh, cp, edge, uo, vo, wo, po, go, ss, ps, us, vs, ws, qs, gs, order_s, sem):
@@ -465,14 +474,17 @@
     def swap_levels(x):
         return lax.all_to_all(x.reshape(8, -1, LANES), "lev", 0, 0, tiled=True, axis_index_groups=[list(ORDER)]).reshape(-1, LANES)
 
-    u, v, w, g, p, m, r, ta, tb, st, index = call(
-        k_init, "init", [order, p, lm, u, v, w, g, flat(stiffness)], [16] * 7 + [15, 15, 16, 0], [16] * 10, hbm_in=8
+    u, v, w, g, p, m, r, ta, st, index = call(
+        k_init, "init", [order, p, lm, u, v, w, g, flat(stiffness)], [16] * 7 + [15, 16, 0], [16] * 6, hbm_in=8
     )
     mn = r3 = None
     statics = None
     for step in range(SUBSTEPS):
         first = step == 0
         ra = lax.ppermute(ta, "elem", mates)
+        u, v, w, g, tb = call(
+            functools.partial(k_rest, first), "rest", [u, v, w, g, p, m, r], [16] * 4 + [15 if first else 12]
+        )
         if first:
             f3, bm, r3 = call(functools.partial(k_b, True), "b1", [u, v, w, g, m, r, ta, ra, tb], [16, 19, 4])
         else:
@@ -501,8 +513,8 @@
         p, vm = call(k_d, "d", [p, w, r, rd, wu, pu, wd, pd, edge], [16, 16])
         rv = swap_levels(vm)
         if step < SUBSTEPS - 1:
-            u, v, w, g, p, ta, tb = call(
-                k_e, "e", [p, w, g, u, v, rv] + statics + [m, r], [16] * 5 + [12, 12], [16] * 4
+            w, g, p, ta = call(
+                k_e, "e", [p, w, g, u, v, rv] + statics + [m, r], [16] * 3 + [12], [16] * 2
             )
         else:
             outs = call(k_out, "out", [order, p, w, g, u, v, rv] + statics, [16] * 5, [16] * 7, hbm_in=1, free_out=True)

time: 142 us -> 142 us (level)
    pallas_call x15 -> x18, Pallas kernels: 8.71 us -> 8.83 us  [call(): pl.pallas_call(kernel, out_shape=[kind((n * NL, LANES), F32) if n else ki...]
  transfers between devices with their start and end apart: 10 -> 10, of which waited for: 8 -> 8; matrix products, arithmetic and copies ran while one was open for 0% -> 0% of each run, Pallas kernels for 1% -> 2%
where the time goes in v5:
time: 142 us; the launch traced here: 141 us
  starting transfers between devices  66.9 us (47%)
  blocking collectives  43.5 us (31%)
  waiting for transfers between devices  21.1 us (15%)
  Pallas kernels  8.83 us (6%)
    ppermute x3, starting transfers between devices, body(): rb = lax.ppermute(bm, 'elem', others)  48.6 us
    all_to_all x3, blocking collectives, swap_levels(): lax.all_to_all(x.reshape(8, -1, LANES), 'lev', 0, 0, tiled=True, axis_ind...  43.5 us
    ppermute x3, waiting for transfers between devices, body(): rb = lax.ppermute(bm, 'elem', others)  11.4 us
    pallas_call x18, Pallas kernels, call(): pl.pallas_call(kernel, out_shape=[kind((n * NL, LANES), F32) if n else ki...  8.83 us
    all_to_all x1, starting transfers between devices, swap_levels(): lax.all_to_all(x.reshape(8, -1, LANES), 'lev', 0, 0, tiled=True, axis_ind...  6.75 us
    ppermute x3, starting transfers between devices, body(): ra = lax.ppermute(ta, 'elem', mates)  5.76 us
    ppermute x3, starting transfers between devices, body(): rd = lax.ppermute(dm, 'elem', mates)  5.76 us
    all_to_all x1, waiting for transfers between devices, swap_levels(): lax.all_to_all(x.reshape(8, -1, LANES), 'lev', 0, 0, tiled=True, axis_ind...  4.33 us
  transfers between devices with their start and end apart: 10, of which 8 were waited for; matrix products, arithmetic and copies ran while one was open for 0% of the time, Pallas kernels for 2%

profile of v5, /device:TPU:32, one launch (start us, length us, event | category | flops | bytes accessed | tf_op | source)
XLA Modules:
  0.0 141.1 jit_solution(2553741199715726234)
XLA Ops:
  0.6 1.9 %init.1 = (f32[256,128]{1,0:T(8,128)S(1)}, f32[256,128]{1,0:T(8,128)S(1)}, f32[256,128]{1,0:T(8,128)S(1)}, f32[256,128]{1,0:T(8,128)S(1)}, f32[256,128]{1,0:T(8,...) custom-call(s32[1,128]{1,0:T(1,128)} %order.3, ...), custom_call_target="tpu_custom_call" | custom-call | tf_op jit(solution)/shard_map/init/pallas_call | solution.py:456
  2.5 1.9 %collective-permute-start = (f32[240,128]{1,0:T(8,128)S(1)}, f32[240,128]{1,0:T(8,128)S(1)}, u32[]{:S(2)}, u32[]{:S(2)}) collective-permute-start(f32[240,128]{1,0:T(8,128)S(1)} %get-tuple-element.96.refs_6_), channel_id=1, source_target_pairs={{0,8},{8,0},{16,24},{24,16},{32,40},{40,32},{48,56},{56,48},{64,72... | collective-permute-start | bytes 368648 | tf_op jit(solution)/shard_map/ppermute | solution.py:484
  4.7 1.1 collective-permute-done.refs_7_
  5.9 19.2 %collective-permute-start.1 = (f32[304,128]{1,0:T(8,128)S(1)}, f32[304,128]{1,0:T(8,128)S(1)}, u32[]{:S(2)}, u32[]{:S(2)}) collective-permute-start(f32[304,128]{1,0:T(8,128)S(1)} %get-tuple-element.100.after), channel_id=1, source_target_pairs={{0,504},{8,16},{16,8},{24,32},{32,24},{40,48},{48,40},{56,64},{64,... | collective-permute-start | bytes 466952 | tf_op jit(solution)/shard_map/ppermute | solution.py:492
  25.2 1.1 col.1
  26.3 6.8 %all-to-all-start = ((f32[8,48,128]{2,1,0:T(8,128)}), f32[8,48,128]{2,1,0:T(8,128)S(1)}, u32[]{:S(2)}, u32[]{:S(2)}) async-start(f32[8,48,128]{2,1,0:T(8,128)} %bitcast.7), calls=%async_computation | async-start | bytes 393216 | tf_op jit(solution)/shard_map/all_to_all | solution.py:475
  33.0 0.3 c1.1
  33.4 1.9 %collective-permute-start.2 = (f32[1152,128]{1,0:T(8,128)S(1)}, f32[1152,128]{1,0:T(8,128)S(1)}, u32[]{:S(2)}, u32[]{:S(2)}) collective-permute-start(f32[1152,128]{1,0:T(8,128)S(1)} %get-tuple-element.106), channel_id=1, source_target_pairs={{0,8},{8,0},{16,24},{24,16},{32,40},{40,32},{48,56},{56,48},{64,72... | collective-permute-start | bytes 1769480 | tf_op jit(solution)/shard_map/ppermute | solution.py:507
  35.3 4.3 %all-to-all-done = f32[8,48,128]{2,1,0:T(8,128)S(1)} async-done(((f32[8,48,128]{2,1,0:T(8,128)}), f32[8,48,128]{2,1,0:T(8,128)S(1)}, u32[]{:S(2)}, u32[]{:S(2)}) %all-to-all-start) | async-done | bytes 196640 | tf_op jit(solution)/shard_map/all_to_all | solution.py:475
  39.8 0.3 d.3
  40.1 13.1 %all_to_all.20 = f32[8,32,128]{2,1,0:T(8,128)S(1)} all-to-all(f32[8,32,128]{2,1,0:T(8,128)S(1)} %bitcast.25), channel_id=1, replica_groups={{4,0,7,1,6,2,5,3},{12,8,15,9,14,10,13,11},{20,16,23,17,22,18,21,19},{28..., dimensions={0} | all-to-all | bytes 262144 | tf_op jit(solution)/shard_map/all_to_all | solution.py:475
  53.2 0.4 e.2
  53.6 1.9 %collective-permute-start.3 = (f32[192,128]{1,0:T(8,128)S(1)}, f32[192,128]{1,0:T(8,128)S(1)}, u32[]{:S(2)}, u32[]{:S(2)}) collective-permute-start(f32[192,128]{1,0:T(8,128)S(1)} %get-tuple-element.129.refs_6_), channel_id=1, source_target_pairs={{0,8},{8,0},{16,24},{24,16},{32,40},{40,32},{48,56},{56,48},{64,72... | collective-permute-start | bytes 294920 | tf_op jit(solution)/shard_map/ppermute | solution.py:484
  55.6 0.2 rest.4
  55.8 1.0 collective-permute-done.3.refs_7_
  57.0 14.6 %collective-permute-start.4 = (f32[240,128]{1,0:T(8,128)S(1)}, f32[240,128]{1,0:T(8,128)S(1)}, u32[]{:S(2)}, u32[]{:S(2)}) collective-permute-start(f32[240,128]{1,0:T(8,128)S(1)} %get-tuple-element.132), channel_id=1, source_target_pairs={{0,504},{8,16},{16,8},{24,32},{32,24},{40,48},{48,40},{56,64},{64,... | collective-permute-start | bytes 368648 | tf_op jit(solution)/shard_map/ppermute | solution.py:492
  71.6 5.6 %collective-permute-done.4.refs_10_ = f32[240,128]{1,0:T(8,128)S(1)} collective-permute-done((f32[240,128]{1,0:T(8,128)S(1)}, f32[240,128]{1,0:T(8,128)S(1)}, u32[]{:S(2)}, u32[]{:S(2)}) %collective-permute-start.4) | collective-permute-done | bytes 122912 | tf_op jit(solution)/shard_map/ppermute | solution.py:492
  77.2 0.2 c.2
  77.5 1.9 %collective-permute-start.5 = (f32[48,128]{1,0:T(8,128)S(1)}, f32[48,128]{1,0:T(8,128)S(1)}, u32[]{:S(2)}, u32[]{:S(2)}) collective-permute-start(f32[48,128]{1,0:T(8,128)S(1)} %get-tuple-element.137), channel_id=1, source_target_pairs={{0,8},{8,0},{16,24},{24,16},{32,40},{40,32},{48,56},{56,48},{64,72... | collective-permute-start | bytes 73736 | tf_op jit(solution)/shard_map/ppermute | solution.py:507
  79.4 1.2 collective-permute-done.5.rd
  80.8 14.8 %all_to_all.21 = f32[8,32,128]{2,1,0:T(8,128)S(1)} all-to-all(f32[8,32,128]{2,1,0:T(8,128)S(1)} %bitcast.26), channel_id=1, replica_groups={{4,0,7,1,6,2,5,3},{12,8,15,9,14,10,13,11},{20,16,23,17,22,18,21,19},{28..., dimensions={0} | all-to-all | bytes 262144 | tf_op jit(solution)/shard_map/all_to_all | solution.py:475
  95.7 0.4 e.3
  96.1 1.9 %collective-permute-start.6 = (f32[192,128]{1,0:T(8,128)S(1)}, f32[192,128]{1,0:T(8,128)S(1)}, u32[]{:S(2)}, u32[]{:S(2)}) collective-permute-start(f32[192,128]{1,0:T(8,128)S(1)} %get-tuple-element.148.refs_6_), channel_id=1, source_target_pairs={{0,8},{8,0},{16,24},{24,16},{32,40},{40,32},{48,56},{56,48},{64,72... | collective-permute-start | bytes 294920 | tf_op jit(solution)/shard_map/ppermute | solution.py:484
  98.0 0.2 rest.5
  98.2 1.0 collective-permute-done.6.refs_7_
  99.4 14.8 %collective-permute-start.7 = (f32[240,128]{1,0:T(8,128)S(1)}, f32[240,128]{1,0:T(8,128)S(1)}, u32[]{:S(2)}, u32[]{:S(2)}) collective-permute-start(f32[240,128]{1,0:T(8,128)S(1)} %get-tuple-element.151), channel_id=1, source_target_pairs={{0,504},{8,16},{16,8},{24,32},{32,24},{40,48},{48,40},{56,64},{64,... | collective-permute-start | bytes 368648 | tf_op jit(solution)/shard_map/ppermute | solution.py:492
  114.2 5.7 %collective-permute-done.7.refs_10_ = f32[240,128]{1,0:T(8,128)S(1)} collective-permute-done((f32[240,128]{1,0:T(8,128)S(1)}, f32[240,128]{1,0:T(8,128)S(1)}, u32[]{:S(2)}, u32[]{:S(2)}) %collective-permute-start.7) | collective-permute-done | bytes 122912 | tf_op jit(solution)/shard_map/ppermute | solution.py:492
  120.0 0.2 c.3
  120.2 1.9 %collective-permute-start.8 = (f32[48,128]{1,0:T(8,128)S(1)}, f32[48,128]{1,0:T(8,128)S(1)}, u32[]{:S(2)}, u32[]{:S(2)}) collective-permute-start(f32[48,128]{1,0:T(8,128)S(1)} %get-tuple-element.154), channel_id=1, source_target_pairs={{0,8},{8,0},{16,24},{24,16},{32,40},{40,32},{48,56},{56,48},{64,72... | collective-permute-start | bytes 73736 | tf_op jit(solution)/shard_map/ppermute | solution.py:507
  122.1 1.2 collective-permute-done.8.rd
  123.5 15.5 %all_to_all.22 = f32[8,32,128]{2,1,0:T(8,128)S(1)} all-to-all(f32[8,32,128]{2,1,0:T(8,128)S(1)} %bitcast.24), channel_id=1, replica_groups={{4,0,7,1,6,2,5,3},{12,8,15,9,14,10,13,11},{20,16,23,17,22,18,21,19},{28..., dimensions={0} | all-to-all | bytes 262144 | tf_op jit(solution)/shard_map/all_to_all | solution.py:475
  139.1 2.1 %out.1 = (f32[256,128]{1,0:T(8,128)}, f32[256,128]{1,0:T(8,128)}, f32[256,128]{1,0:T(8,128)}, f32[256,128]{1,0:T(8,128)}, f32[256,128]{1,0:T(8,128)}) custom-call(s32[1,128]{1,0:T(1,128)} %order.3, f32[256,128]{1,0:T(8,128)S(1)} %get-tuple-element.155.p, f32[256,128]{1,0:T(8,128)S(1)} %get-tuple-element.153.w, f32[256,128]{1,0:T(8,128)S(1)} %get-tuple-element.156.g, ...), custom_call_target="tpu_custom_call" | custom-call | tf_op jit(solution)/shard_map/out/pallas_call | solution.py:456
  (9 shorter events, 1.3 us)
Async XLA Ops:
  2.5 3.2 %collective-permute-start = (f32[240,128]{1,0:T(8,128)S(1)}, f32[240,128]{1,0:T(8,128)S(1)}, u32[]{:S(2)}, u32[]{:S(2)}) collective-permute-start(f32[240,128]{1,0:T(8,128)S(1)} %get-tuple-element.96.refs_6_), channel_id=1, source_target_pairs={{0,8},{8,0},{16,24},{24,16},{32,40},{40,32},{48,56},{56,48},{64,72... | collective-permute-start | bytes 368648 | tf_op jit(solution)/shard_map/ppermute | solution.py:484
  5.9 27.1 %collective-permute-start.1 = (f32[304,128]{1,0:T(8,128)S(1)}, f32[304,128]{1,0:T(8,128)S(1)}, u32[]{:S(2)}, u32[]{:S(2)}) collective-permute-start(f32[304,128]{1,0:T(8,128)S(1)} %get-tuple-element.100.after), channel_id=1, source_target_pairs={{0,504},{8,16},{16,8},{24,32},{32,24},{40,48},{48,40},{56,64},{64,... | collective-permute-start | bytes 466952 | tf_op jit(solution)/shard_map/ppermute | solution.py:492
  26.3 13.3 %all-to-all-start = ((f32[8,48,128]{2,1,0:T(8,128)}), f32[8,48,128]{2,1,0:T(8,128)S(1)}, u32[]{:S(2)}, u32[]{:S(2)}) async-start(f32[8,48,128]{2,1,0:T(8,128)} %bitcast.7), calls=%async_computation | async-start | bytes 393216 | tf_op jit(solution)/shard_map/all_to_all | solution.py:475
  33.4 6.3 %collective-permute-start.2 = (f32[1152,128]{1,0:T(8,128)S(1)}, f32[1152,128]{1,0:T(8,128)S(1)}, u32[]{:S(2)}, u32[]{:S(2)}) collective-permute-start(f32[1152,128]{1,0:T(8,128)S(1)} %get-tuple-element.106), channel_id=1, source_target_pairs={{0,8},{8,0},{16,24},{24,16},{32,40},{40,32},{48,56},{56,48},{64,72... | collective-permute-start | bytes 1769480 | tf_op jit(solution)/shard_map/ppermute | solution.py:507
  53.6 3.2 %collective-permute-start.3 = (f32[192,128]{1,0:T(8,128)S(1)}, f32[192,128]{1,0:T(8,128)S(1)}, u32[]{:S(2)}, u32[]{:S(2)}) collective-permute-start(f32[192,128]{1,0:T(8,128)S(1)} %get-tuple-element.129.refs_6_), channel_id=1, source_target_pairs={{0,8},{8,0},{16,24},{24,16},{32,40},{40,32},{48,56},{56,48},{64,72... | collective-permute-start | bytes 294920 | tf_op jit(solution)/shard_map/ppermute | solution.py:484
  57.0 20.3 %collective-permute-start.4 = (f32[240,128]{1,0:T(8,128)S(1)}, f32[240,128]{1,0:T(8,128)S(1)}, u32[]{:S(2)}, u32[]{:S(2)}) collective-permute-start(f32[240,128]{1,0:T(8,128)S(1)} %get-tuple-element.132), channel_id=1, source_target_pairs={{0,504},{8,16},{16,8},{24,32},{32,24},{40,48},{48,40},{56,64},{64,... | collective-permute-start | bytes 368648 | tf_op jit(solution)/shard_map/ppermute | solution.py:492
  77.5 3.1 %collective-permute-start.5 = (f32[48,128]{1,0:T(8,128)S(1)}, f32[48,128]{1,0:T(8,128)S(1)}, u32[]{:S(2)}, u32[]{:S(2)}) collective-permute-start(f32[48,128]{1,0:T(8,128)S(1)} %get-tuple-element.137), channel_id=1, source_target_pairs={{0,8},{8,0},{16,24},{24,16},{32,40},{40,32},{48,56},{56,48},{64,72... | collective-permute-start | bytes 73736 | tf_op jit(solution)/shard_map/ppermute | solution.py:507
  96.1 3.2 %collective-permute-start.6 = (f32[192,128]{1,0:T(8,128)S(1)}, f32[192,128]{1,0:T(8,128)S(1)}, u32[]{:S(2)}, u32[]{:S(2)}) collective-permute-start(f32[192,128]{1,0:T(8,128)S(1)} %get-tuple-element.148.refs_6_), channel_id=1, source_target_pairs={{0,8},{8,0},{16,24},{24,16},{32,40},{40,32},{48,56},{56,48},{64,72... | collective-permute-start | bytes 294920 | tf_op jit(solution)/shard_map/ppermute | solution.py:484
  99.4 20.5 %collective-permute-start.7 = (f32[240,128]{1,0:T(8,128)S(1)}, f32[240,128]{1,0:T(8,128)S(1)}, u32[]{:S(2)}, u32[]{:S(2)}) collective-permute-start(f32[240,128]{1,0:T(8,128)S(1)} %get-tuple-element.151), channel_id=1, source_target_pairs={{0,504},{8,16},{16,8},{24,32},{32,24},{40,48},{48,40},{56,64},{64,... | collective-permute-start | bytes 368648 | tf_op jit(solution)/shard_map/ppermute | solution.py:492
  120.2 3.1 %collective-permute-start.8 = (f32[48,128]{1,0:T(8,128)S(1)}, f32[48,128]{1,0:T(8,128)S(1)}, u32[]{:S(2)}, u32[]{:S(2)}) collective-permute-start(f32[48,128]{1,0:T(8,128)S(1)} %get-tuple-element.154), channel_id=1, source_target_pairs={{0,8},{8,0},{16,24},{24,16},{32,40},{40,32},{48,56},{56,48},{64,72... | collective-permute-start | bytes 73736 | tf_op jit(solution)/shard_map/ppermute | solution.py:507
